TPU v7x, 128 devices: a whole 4x4x4 slice. The times are simulated.
128 devices in a mesh: grp: 8 (over y, z_lo), tp: 16 (over z_hi, x, core).
Axes of the slice: x: 4, y: 4, z: 4 (z_hi: 2, z_lo: 2; z = z_hi * 2 + z_lo), core: 2. Of those that a mesh axis runs over, the one named last changes fastest.
Arguments:
- features: bfloat16 [2048, 49152], P('grp', 'tp'), may hold values from -24 to 24
- weight: bfloat16 [49152, 8192], P('tp', 'grp'), may hold values from -0.049804688 to 0.049804688
- norm_gain: float32 [8192], P('grp'), may hold values from 0.1 to 1.9
- target: bfloat16 [2048, 8192], P(None, 'grp'), may hold values from -6 to 6
- counts: int32 [256], replicated, may hold values from 1 to 8
Outputs:
- weight_grad: bfloat16 [49152, 8192], P('tp', 'grp')
- draft_loss: float32 [], replicated
All inputs are finite; a program needn't handle non-finite values.
Results may differ from a plain program's by a relative error of at most 0.0085.
Values may be sent and summed in bfloat16 or wider, within the bound.
A program may use at most 128 MiB of HBM per device.

v0:
```python
import jax
import jax.numpy as jnp
from jax import lax
from jax.sharding import PartitionSpec as P

DOUT = 8192
SPEC = 8


epsilon = 1e-06


def row_mask(counts, row_start, row_count):
    row_index = row_start + jnp.arange(row_count, dtype=jnp.int32)
    owner = jnp.take(counts, row_index // SPEC)
    return (row_index % SPEC < owner).astype(jnp.float32)[:, None]


def backward_rows(hidden, target_rows, row_live, norm_gain, accepted):
    gain_row = norm_gain[None, :]
    squares = lax.psum(jnp.sum(hidden * hidden, axis=1), "grp")
    inverse_rms = lax.rsqrt(squares / DOUT + epsilon)[:, None]
    normed = hidden * inverse_rms * gain_row
    deviation = normed - target_rows
    residual = row_live * deviation / accepted
    coupling = lax.psum(jnp.sum(gain_row * residual * hidden, axis=1), "grp")[:, None]
    act_grad = (
        inverse_rms * gain_row * residual - hidden * inverse_rms**3 * coupling / DOUT
    ).astype(jnp.bfloat16)
    partial_loss = 0.5 * jnp.sum(residual * deviation)
    return (act_grad, partial_loss)


def shards(features, weight, norm_gain, target, counts):
    gathered = lax.all_gather(features, "grp", axis=0, tiled=True)
    total_rows = gathered.shape[0]
    accepted = jnp.sum(counts).astype(jnp.float32)
    rows_here = total_rows // lax.axis_size("tp")
    row_start = lax.axis_index("tp") * rows_here
    hidden = lax.psum_scatter(
        jnp.dot(gathered, weight, preferred_element_type=jnp.float32).astype(jnp.bfloat16),
        "tp",
        scatter_dimension=0,
        tiled=True,
    ).astype(jnp.float32)
    target_rows = lax.dynamic_slice_in_dim(target, row_start, rows_here, 0).astype(jnp.float32)
    row_live = row_mask(counts, row_start, rows_here)
    act_grad, partial_loss = backward_rows(hidden, target_rows, row_live, norm_gain, accepted)
    all_grad = lax.all_gather(act_grad, "tp", axis=0, tiled=True)
    draft_loss = lax.psum(partial_loss, ("grp", "tp"))
    weight_grad = lax.dot_general(
        gathered, all_grad, (((0,), (0,)), ((), ())), preferred_element_type=jnp.float32
    ).astype(jnp.bfloat16)
    return (weight_grad, draft_loss)


def solution(mesh):
    placed = (P("grp", "tp"), P("tp", "grp"), P("grp"), P(None, "grp"), P())
    return jax.shard_map(
        shards, mesh=mesh, in_specs=placed, out_specs=(P("tp", "grp"), P()), check_vma=False
    )
```

profile of v0, /device:TPU:1, one launch (start us, length us, event | category | flops | bytes accessed | tf_op | source)
XLA Modules:
  0.0 507.1 jit_solution(5090543502613461760)
XLA Ops:
  7.2 0.0 all-gather.3.cloned.1.call-start
  7.2 0.7 all-gather.3.cloned.1.call-update
  7.9 0.0 copy-start
  7.9 0.0 copy-start.1
  7.9 0.0 reduce-scatter.2.cloned.1.call-start
  8.0 251.7 %all-gather.3.cloned.1.call-done = bf16[2048,3072]{1,0:T(8,128)(2,1)} async-done(((bf16[256,3072]{1,0:T(8,128)(2,1)}), bf16[2048,3072]{1,0:T(8,128)(2,1)}) %all-gather.3.cloned.1.call-update) | async-done | bytes 12582928 | tf_op jit(solution)/shard_map/all_gather | solution.py:35
  259.7 18.8 %convolution_convert_fusion = bf16[2048,1024]{1,0:T(8,128)(2,1)} fusion(bf16[2048,3072]{1,0:T(8,128)(2,1)} %all-gather.3.cloned.1.call-done, bf16[3072,1024]{1,0:T(8,128)(2,1)} %param.6), kind=kOutput, calls=%fused_computation.2 | convolution fusion | flops 12886999040 | bytes 23068672 | tf_op jit(solution)/shard_map/dot_general | solution.py:41
  278.5 0.0 reduce-scatter.2.cloned.1.call-update
  278.5 0.0 all-gather.5.cloned.1.call-start
  278.5 0.0 copy-done
  278.5 0.6 reduce_sum.37
  279.9 1.3 gather_fusion
  281.2 77.8 %reduce-scatter.2.cloned.1.call-done = bf16[128,1024]{1,0:T(8,128)(2,1)} async-done(((bf16[2048,1024]{1,0:T(8,128)(2,1)}), bf16[128,1024]{1,0:T(8,128)(2,1)}) %reduce-scatter.2.cloned.1.call-update) | async-done | bytes 262160 | tf_op jit(solution)/shard_map/reduce_scatter | solution.py:40
  359.0 1.1 fusion
  360.1 15.3 %psum.21 = f32[128]{0:T(128)S(1)} all-reduce(f32[128]{0:T(128)S(1)} %fusion), channel_id=1, replica_groups=mesh['grp'=8,'tp'=16] {'grp'}, use_global_device_ids=true, to_apply=%region_2.3 | all-reduce | flops 128 | bytes 1024 | tf_op jit(solution)/shard_map/psum | solution.py:21
  375.4 0.0 copy-done.1
  375.4 2.0 multiply_reduce_fusion
  377.4 12.5 %psum.22 = f32[128]{0:T(128)S(1)} all-reduce(f32[128]{0:T(128)S(1)} %get-tuple-element.7), channel_id=1, replica_groups=mesh['grp'=8,'tp'=16] {'grp'}, use_global_device_ids=true, to_apply=%region_5.6 | all-reduce | flops 128 | bytes 1024 | tf_op jit(solution)/shard_map/psum | solution.py:26
  389.9 2.0 fusion.6
  391.9 0.0 all-gather.5.cloned.1.call-update
  392.6 80.8 %psum.23 = f32[]{:T(128)} all-reduce(f32[]{:T(128)S(6)} %mul_shard_map.3), channel_id=1, replica_groups=mesh['grp'=8,'tp'=16] {'grp','tp'}, use_global_device_ids=true, to_apply=%region_7.8 | all-reduce | flops 1 | bytes 8 | tf_op jit(solution)/shard_map/psum | solution.py:50
  473.4 0.0 all-gather.5.cloned.1.call-done
  473.4 18.6 %convert_bitcast_fusion = bf16[3072,1024]{0,1:T(8,128)(2,1)} fusion(bf16[2048,1024]{1,0:T(8,128)(2,1)} %all-gather.5.cloned.1.call-done, bf16[2048,3072]{1,0:T(8,128)(2,1)} %all-gather.3.cloned.1.call-done), kind=kOutput, calls=%fused_computation.1 | convolution fusion | flops 12888047616 | bytes 23068672 | tf_op jit(solution)/shard_map/dot_general | solution.py:51
  492.0 8.6 %copy.8 = bf16[3072,1024]{1,0:T(8,128)(2,1)} copy(bf16[3072,1024]{0,1:T(8,128)(2,1)} %convert_bitcast_fusion) | data formatting | bytes 12582912
  (4 shorter events, 0.0 us)
Async XLA Ops:
  7.2 252.5 %all-gather.3.cloned.1.call-start = ((), (), s32[]{:S(2)}) async-start(), calls=%async_computation.1 | async-start | bytes 14155776 | tf_op jit(solution)/shard_map/all_gather | solution.py:35
  7.9 270.6 %copy-start = (s32[256]{0:T(256)S(1)}, s32[256]{0:T(256)}, u32[]{:S(2)}) copy-start(s32[256]{0:T(256)} %param.9) | copy-start | bytes 3076
  7.9 367.5 %copy-start.1 = (f32[1024]{0:T(1024)S(1)}, f32[1024]{0:T(1024)}, u32[]{:S(2)}) copy-start(f32[1024]{0:T(1024)} %param.7) | copy-start | bytes 12292
  7.9 351.1 %reduce-scatter.2.cloned.1.call-start = ((), (), s32[]{:S(2)}) async-start(), calls=%async_computation.2 | async-start | bytes 4456448 | tf_op jit(solution)/shard_map/reduce_scatter | solution.py:40
  278.5 194.9 %all-gather.5.cloned.1.call-start = ((), (), s32[]{:S(2)}) async-start(), calls=%async_computation.3 | async-start | bytes 4456448 | tf_op jit(solution)/shard_map/all_gather | solution.py:49
Sparse Core Ops, SparseCore 0:
  9.6 250.0 all-gather.2
  278.6 80.3 reduce-scatter.1
  392.1 62.8 all-gather.4
where the time goes:
time: 508 us; the launch traced here: 507 us
  waiting for transfers between devices  330 us (65%)
  blocking collectives  109 us (21%)
  matrix products  37.4 us (7%)
  between operations  15.1 us (3%)
  local copies, waits for them, and re-layouts  9.89 us (2%)
  other arithmetic  5.84 us (1%)
    all_gather x1, waiting for transfers between devices, shards(): gathered = lax.all_gather(features, 'grp', axis=0, tiled=True)  252 us
    psum x1, blocking collectives, shards(): draft_loss = lax.psum(partial_loss, ('grp', 'tp'))  80.8 us
    reduce_scatter x1, waiting for transfers between devices, shards(): lax.psum_scatter(jnp.dot(gathered, weight, preferred_element_type=jnp.flo...  77.8 us
    dot_general x1, matrix products, shards(): jnp.dot(gathered, weight, preferred_element_type=jnp.float32)  18.8 us
    dot_general x1, matrix products, shards(): lax.dot_general(gathered, all_grad, (((0,), (0,)), ((), ())), preferred_e...  18.6 us
    psum x1, blocking collectives, backward_rows(): squares = lax.psum(jnp.sum(hidden * hidden, axis=1), 'grp')  15.3 us
    psum x1, blocking collectives, backward_rows(): lax.psum(jnp.sum(gain_row * residual * hidden, axis=1), 'grp')[:, None]  12.5 us
  transfers between devices with their start and end apart: 3, of which 2 were waited for; matrix products, arithmetic and copies ran while one was open for 0% of the time, Pallas kernels for 0%

commit v1 on v0

v1 whole, which is shorter than its diff:
```python
import functools

import jax
import jax.numpy as jnp
from jax import lax
from jax.experimental import pallas as pl
from jax.experimental.pallas import tpu as pltpu
from jax.sharding import PartitionSpec as P

SPEC = 8
EPS = 1e-06
CHUNKS = (64, 64, 64, 64)
TILE = 256
MESH = pl.DeviceIdType.MESH

TP_OFF = ((0, 1), (0, 3), (0, 2), (1, 0), (1, 1), (1, 3), (1, 2))
GRP_OFF = ((0, 1), (1, 0), (3, 0), (2, 0), (1, 1), (3, 1), (2, 1))


def kernel(
    dout, split, features, weight, gain_ref, target, counts_s, counts_v, out, loss_out,
    fbuf, wbuf, acc, gbuf, stage, hsend, hrecv, hown, hsum, rsrecv, hid, tgt,
    st_own, st_recv, loss_acc, l1_recv, l2_own, l2_recv,
    w_sem, f_sem, t_sem, o_sem,
    ag_s, ag_r, hp_s, hp_r, rs_s, rs_r, st_s, st_r, ga_s, ga_r, gp_s, gp_r,
    l1_s, l1_r, l2_s, l2_r,
):
    g, t = lax.axis_index("grp"), lax.axis_index("tp")
    y, zl = g // 2, lax.rem(g, 2)
    core, q = lax.rem(t, 2), t // 2
    zh, x = q // 4, lax.rem(q, 4)
    depth, cols = wbuf.shape
    rows_g = features.shape[0]
    n_chunks = len(CHUNKS)
    offs = [sum(CHUNKS[:c]) for c in range(n_chunks)]
    a_cols, a_half, half = split

    def grp_dev(dy, dz):
        return lax.rem(y + dy, 4) * 2 + lax.rem(zl + dz, 2)

    def chip(dz, dx):
        return lax.rem(zh + dz, 2) * 4 + lax.rem(x + dx, 4)

    zp, yp, ym, yo = grp_dev(0, 1), grp_dev(1, 0), grp_dev(3, 0), grp_dev(2, 0)
    zyp, zym, zyo = grp_dev(1, 1), grp_dev(3, 1), grp_dev(2, 1)
    other = t + 1 - 2 * core

    tp_peers = [chip(*o) * 2 + core for o in TP_OFF]
    grp_peers = [grp_dev(*o) for o in GRP_OFF]
    all_tp = tp_peers + [chip(*o) * 2 + 1 - core for o in TP_OFF] + [other]

    barrier = pltpu.get_barrier_semaphore()
    for p in grp_peers:
        pl.semaphore_signal(barrier, inc=1, device_id=(p, t), device_id_type=MESH)
    for p in all_tp:
        pl.semaphore_signal(barrier, inc=1, device_id=(g, p), device_id_type=MESH)

    sends = []

    def remote(src, dst, ssem, rsem, dev):
        cp = pltpu.make_async_remote_copy(
            src_ref=src, dst_ref=dst, send_sem=ssem, recv_sem=rsem, device_id=dev, device_id_type=MESH
        )
        cp.start()
        sends.append(cp)

    def arrived(dst, ssem, rsem):
        pltpu.make_async_remote_copy(
            src_ref=dst, dst_ref=dst, send_sem=ssem, recv_sem=rsem, device_id=(zp, t), device_id_type=MESH
        ).wait_recv()

    local = []
    for c in range(n_chunks):
        r = CHUNKS[c]
        cp = pltpu.make_async_copy(
            features.at[pl.ds(offs[c], r), :],
            fbuf.at[pl.ds(pl.multiple_of(8 * offs[c] + g * r, 16), r), :],
            f_sem.at[c],
        )
        cp.start()
        local.append(cp)
    w_cp = pltpu.make_async_copy(weight, wbuf, w_sem)
    w_cp.start()

    def own_rows(c):
        r = CHUNKS[c]
        return (core * 4 + q // 2) * rows_g + offs[c] + lax.rem(q, 2) * (r // 2)

    t_cps = []
    for c in range(n_chunks):
        r = CHUNKS[c]
        cp = pltpu.make_async_copy(
            target.at[pl.ds(pl.multiple_of(own_rows(c), 16), r // 2), :],
            tgt.at[pl.ds(4 * 0 + offs[c] // 2, r // 2), :],
            t_sem.at[c],
        )
        cp.start()
        t_cps.append(cp)

    pl.semaphore_wait(barrier, len(grp_peers) + len(all_tp))

    def seg(c, who, lo, n):
        r = CHUNKS[c]
        return fbuf.at[pl.ds(pl.multiple_of(8 * offs[c] + who * r, 16), r), pl.ds(lo, n)]

    def ag_put(c, k, who, lo, n, dev):
        remote(seg(c, who, lo, n), seg(c, who, lo, n), ag_s.at[c, k], ag_r.at[c, k], (dev, t))

    def ag_own(c, k, lo, n, dev):
        r = CHUNKS[c]
        remote(
            features.at[pl.ds(offs[c], r), pl.ds(lo, n)], seg(c, g, lo, n),
            ag_s.at[c, k], ag_r.at[c, k], (dev, t),
        )

    def ag_got(c, k, who, lo, n):
        arrived(seg(c, who, lo, n), ag_s.at[c, k], ag_r.at[c, k])

    b_cols = depth - a_cols

    def start(c):
        ag_own(c, 0, 0, a_cols, zp)
        ag_own(c, 1, 0, depth, yp)
        ag_own(c, 2, 0, depth, ym)
        ag_own(c, 3, a_cols, b_cols, zp)

    def round1(c):
        ag_got(c, 0, zp, 0, a_cols)
        ag_put(c, 4, zp, 0, a_cols, yp)
        ag_put(c, 5, zp, 0, a_cols, ym)

    def round2(c):
        ag_got(c, 1, ym, 0, depth)
        ag_put(c, 6, ym, 0, half, yp)
        ag_put(c, 10, ym, a_cols, b_cols, zp)
        ag_got(c, 2, yp, 0, depth)
        ag_put(c, 7, yp, half, depth - half, ym)
        ag_put(c, 11, yp, a_cols, b_cols, zp)

    def round3(c):
        ag_got(c, 4, zym, 0, a_cols)
        ag_put(c, 8, zym, 0, a_half, yp)
        ag_got(c, 5, zyp, 0, a_cols)
        ag_put(c, 9, zyp, a_half, a_cols - a_half, ym)

    def round4(c):
        ag_got(c, 6, yo, 0, half)
        ag_got(c, 7, yo, half, depth - half)
        ag_put(c, 12, yo, a_cols, b_cols, zp)

    def finish(c):
        ag_got(c, 3, zp, a_cols, b_cols)
        ag_got(c, 10, zym, a_cols, b_cols)
        ag_got(c, 11, zyp, a_cols, b_cols)
        ag_got(c, 8, zyo, 0, a_half)
        ag_got(c, 9, zyo, a_half, a_cols - a_half)
        ag_got(c, 12, zyo, a_cols, b_cols)
        local[c].wait()

    def matmul_half(c, which, keep):
        r4 = 4 * CHUNKS[c]
        start_row = pl.multiple_of(8 * offs[c] + which * r4, 16)

        def tile(n, _):
            col = pl.ds(pl.multiple_of(n * TILE, TILE), TILE)
            part = jnp.dot(
                fbuf[pl.ds(start_row, r4), :], wbuf[:, col], preferred_element_type=jnp.float32
            )
            if keep:
                hown[pl.ds(0, r4), col] = part
            else:
                hsend[pl.ds(4 * offs[c], r4), col] = part.astype(jnp.bfloat16)
            return 0

        lax.fori_loop(0, cols // TILE, tile, 0)

    def matmul_other(c):
        matmul_half(c, 1 - core, False)
        rows = pl.ds(4 * offs[c], 4 * CHUNKS[c])
        remote(hsend.at[rows, :], hrecv.at[rows, :], hp_s.at[c], hp_r.at[c], (g, other))

    def matmul_mine(c):
        matmul_half(c, core, True)

    def spread(c):
        r = CHUNKS[c]
        base = 4 * offs[c]
        arrived(hrecv.at[pl.ds(base, 4 * r), :], hp_s.at[c], hp_r.at[c])

        def add(i, _):
            lo = pl.multiple_of(i * 16, 16)
            both = hown[pl.ds(lo, 16), :] + hrecv[pl.ds(base + lo, 16), :].astype(jnp.float32)
            hsum[pl.ds(base + lo, 16), :] = both.astype(jnp.bfloat16)
            return 0

        lax.fori_loop(0, 4 * r // 16, add, 0)
        n = r // 2
        for k, o in enumerate(TP_OFF):
            remote(
                hsum.at[pl.ds(pl.multiple_of(base + chip(*o) * n, 16), n), :],
                rsrecv.at[k, pl.ds(offs[c] // 2, n), :],
                rs_s.at[c, k], rs_r.at[c, k], (g, tp_peers[k]),
            )

    def stats(c):
        n = CHUNKS[c] // 2
        rows = pl.ds(offs[c] // 2, n)
        mine = pl.multiple_of(q * n, 16)
        h = hown[pl.ds(mine, n), :]
        h = h + hrecv[pl.ds(pl.multiple_of(4 * offs[c] + mine, 16), n), :].astype(jnp.float32)
        for k in range(7):
            arrived(rsrecv.at[k, rows, :], rs_s.at[c, k], rs_r.at[c, k])
            h = h + rsrecv[k, rows, :].astype(jnp.float32)
        hid[pl.ds(0, n), :] = h
        t_cps[c].wait()
        gh = gain_ref[...] * h
        s1 = jnp.sum(h * h, axis=1, keepdims=True)
        s2 = jnp.sum(gh * gh, axis=1, keepdims=True)
        s3 = jnp.sum(gh * tgt[rows, :].astype(jnp.float32), axis=1, keepdims=True)
        lane = lax.broadcasted_iota(jnp.int32, (n, 128), 1)
        st_own[rows, :] = jnp.where(lane == 0, s1, jnp.where(lane == 1, s2, s3))
        for k in range(7):
            remote(
                st_own.at[rows, :], st_recv.at[k, rows, :], st_s.at[c, k], st_r.at[c, k], (grp_peers[k], t)
            )

    def gradient(c):
        n = CHUNKS[c] // 2
        rows = pl.ds(offs[c] // 2, n)
        total = st_own[rows, :]
        for k in range(7):
            arrived(st_recv.at[k, rows, :], st_s.at[c, k], st_r.at[c, k])
            total = total + st_recv[k, rows, :]
        s1, s2, s3 = total[:, 0:1], total[:, 1:2], total[:, 2:3]
        inv = lax.rsqrt(s1 / dout + EPS)
        accepted = jnp.sum(counts_v[...].astype(jnp.float32), keepdims=True)
        first = own_rows(c) // SPEC
        sub = lax.broadcasted_iota(jnp.int32, (SPEC, 128), 0)
        live = jnp.concatenate(
            [(sub < counts_s[first + i]).astype(jnp.float32) for i in range(n // SPEC)], axis=0
        )[:, 0:1]
        scale = live / accepted
        gain = gain_ref[...]
        h = hid[pl.ds(0, n), :]
        dev = h * inv * gain - tgt[rows, :].astype(jnp.float32)
        res = scale * dev
        coupling = scale * (inv * s2 - s3)
        grad = inv * gain * res - h * (inv * inv * inv * coupling / dout)
        mine = pl.ds(pl.multiple_of(8 * offs[c] + core * 4 * CHUNKS[c] + q * n, 16), n)
        gbuf[mine, :] = grad.astype(jnp.bfloat16)
        lost = res * dev
        part = loss_acc[...]
        for i in range(n // 8):
            for j in range(cols // 128):
                part = part + lost[8 * i : 8 * i + 8, 128 * j : 128 * j + 128]
        loss_acc[...] = part
        for k in range(7):
            remote(gbuf.at[mine, :], gbuf.at[mine, :], ga_s.at[c, k], ga_r.at[c, k], (g, tp_peers[k]))
        remote(gbuf.at[mine, :], gbuf.at[mine, :], gp_s.at[c, 7], gp_r.at[c, 7], (g, other))

    def grad_rows(c, who_core, who_chip):
        n = CHUNKS[c] // 2
        return gbuf.at[pl.ds(pl.multiple_of(8 * offs[c] + who_core * 4 * CHUNKS[c] + who_chip * n, 16), n), :]

    def pass_on(c):
        for k, (dz, dx) in enumerate(TP_OFF):
            ref = grad_rows(c, core, chip((2 - dz) % 2, (4 - dx) % 4))
            arrived(ref, ga_s.at[c, k], ga_r.at[c, k])
            remote(ref, ref, gp_s.at[c, k], gp_r.at[c, k], (g, other))

    def other_grads(c):
        arrived(grad_rows(c, 1 - core, q), gp_s.at[c, 7], gp_r.at[c, 7])
        for k, (dz, dx) in enumerate(TP_OFF):
            arrived(grad_rows(c, 1 - core, chip((2 - dz) % 2, (4 - dx) % 4)), gp_s.at[c, k], gp_r.at[c, k])

    n_tiles = depth // TILE
    last = n_chunks - 1

    def outer(c, lo, hi):
        rows = pl.ds(8 * offs[c], 8 * CHUNKS[c])

        def tile(i, _):
            k = pl.ds(pl.multiple_of(i * TILE, TILE), TILE)
            for n in range(cols // TILE):
                col = pl.ds(n * TILE, TILE)
                part = lax.dot_general(
                    fbuf[rows, k], gbuf[rows, col], (((0,), (0,)), ((), ())),
                    preferred_element_type=jnp.float32,
                )
                if c > 0:
                    part = part + acc[k, col]
                if c == last:
                    stage[k, col] = part.astype(jnp.bfloat16)
                else:
                    acc[k, col] = part
            if c == last:
                pltpu.make_async_copy(stage.at[k, :], out.at[k, :], o_sem.at[i]).start()
            return 0

        lax.fori_loop(lo, hi, tile, 0)

    loss_acc[...] = jnp.zeros_like(loss_acc)
    start(0)
    round1(0)
    round2(0)
    if n_chunks > 1:
        start(1)
    round3(0)
    round4(0)
    w_cp.wait()
    finish(0)
    for c in range(n_chunks):
        more = c + 1 < n_chunks
        matmul_other(c)
        if more:
            round1(c + 1)
        matmul_mine(c)
        if more:
            round2(c + 1)
            if c + 2 < n_chunks:
                start(c + 2)
        if c > 0:
            pass_on(c - 1)
        spread(c)
        if more:
            round3(c + 1)
        if c > 0:
            other_grads(c - 1)
            outer(c - 1, 0, n_tiles)
        if more:
            round4(c + 1)
        stats(c)
        gradient(c)
        if more:
            finish(c + 1)
    for k, p in enumerate(all_tp):
        remote(loss_acc, l1_recv.at[k], l1_s.at[k], l1_r.at[k], (g, p))
    pass_on(last)
    sum1 = loss_acc[...]
    for k in range(15):
        arrived(l1_recv.at[k], l1_s.at[k], l1_r.at[k])
        sum1 = sum1 + l1_recv[k]
    l2_own[...] = sum1
    for k in range(7):
        remote(l2_own, l2_recv.at[k], l2_s.at[k], l2_r.at[k], (grp_peers[k], t))
    other_grads(last)
    outer(last, 0, n_tiles)
    sum2 = l2_own[...]
    for k in range(7):
        arrived(l2_recv.at[k], l2_s.at[k], l2_r.at[k])
        sum2 = sum2 + l2_recv[k]
    loss_out[0, 0] = 0.5 * jnp.sum(sum2)
    for i in range(n_tiles):
        k = pl.ds(i * TILE, TILE)
        pltpu.make_async_copy(stage.at[k, :], out.at[k, :], o_sem.at[i]).wait()
    for cp in sends:
        cp.wait_send()


def shards(features, weight, norm_gain, target, counts):
    rows_g, depth = features.shape
    cols = weight.shape[1]
    total = target.shape[0]
    n = len(CHUNKS)
    bf, f32 = jnp.bfloat16, jnp.float32
    own = total // 16
    dma = pltpu.SemaphoreType.DMA
    anyspace = pl.BlockSpec(memory_space=pl.ANY)
    vmem = pl.BlockSpec(memory_space=pltpu.VMEM)
    unit = depth // 128
    a_units = unit * 16 // 24
    split = (a_units * 128, (a_units // 2) * 128, (unit // 2) * 128)
    out, loss = pl.pallas_call(
        functools.partial(kernel, cols * lax.axis_size("grp"), split),
        out_shape=(
            jax.ShapeDtypeStruct((depth, cols), bf),
            jax.ShapeDtypeStruct((1, 1), f32),
        ),
        in_specs=[anyspace, anyspace, vmem, anyspace, pl.BlockSpec(memory_space=pltpu.SMEM), vmem],
        out_specs=(anyspace, pl.BlockSpec(memory_space=pltpu.SMEM)),
        scratch_shapes=[
            pltpu.VMEM((total, depth), bf),
            pltpu.VMEM((depth, cols), bf),
            pltpu.VMEM((depth, cols), f32),
            pltpu.VMEM((total, cols), bf),
            pltpu.VMEM((depth, cols), bf),
            pltpu.VMEM((total // 2, cols), bf),
            pltpu.VMEM((total // 2, cols), bf),
            pltpu.VMEM((4 * max(CHUNKS), cols), f32),
            pltpu.VMEM((total // 2, cols), bf),
            pltpu.VMEM((7, own, cols), bf),
            pltpu.VMEM((max(CHUNKS) // 2, cols), f32),
            pltpu.VMEM((own, cols), bf),
            pltpu.VMEM((own, 128), f32),
            pltpu.VMEM((7, own, 128), f32),
            pltpu.VMEM((8, 128), f32),
            pltpu.VMEM((15, 8, 128), f32),
            pltpu.VMEM((8, 128), f32),
            pltpu.VMEM((7, 8, 128), f32),
            dma, dma((n,)), dma((n,)), dma((depth // TILE,)),
            dma((n, 13)), dma((n, 13)), dma((n,)), dma((n,)), dma((n, 7)), dma((n, 7)),
            dma((n, 7)), dma((n, 7)), dma((n, 7)), dma((n, 7)), dma((n, 8)), dma((n, 8)),
            dma((15,)), dma((15,)), dma((7,)), dma((7,)),
        ],
        compiler_params=pltpu.CompilerParams(
            collective_id=0, has_side_effects=True, vmem_limit_bytes=64 * 1024 * 1024 - 65536
        ),
    )(features, weight, norm_gain.reshape(1, cols), target, counts, counts.reshape(2, -1))
    return out, loss[0, 0]


def solution(mesh):
    placed = (P("grp", "tp"), P("tp", "grp"), P("grp"), P(None, "grp"), P())
    return jax.shard_map(
        shards, mesh=mesh, in_specs=placed, out_specs=(P("tp", "grp"), P()), check_vma=False
    )
```

time: 508 us -> 182 us (0.36)
  waiting for transfers between devices: 330 us -> 0 us
  Pallas kernels: 0 us -> 173 us
  blocking collectives: 109 us -> 0 us
  matrix products: 37.4 us -> 0 us
  between operations: 15.1 us -> 2.4 us
  other arithmetic: 5.84 us -> 0 us
    all_gather x2 -> x0, waiting for transfers between devices: 252 us -> none  [the longest x1 252 us: shards(): gathered = lax.all_gather(features, 'grp', axis=0, tiled=True)]
    pallas_call x0 -> x1, Pallas kernels: none -> 173 us  [shards(): pl.pallas_call(functools.partial(kernel, cols * lax.axis_size('grp'), spl...]
    psum x3 -> x0, blocking collectives: 109 us -> none  [the longest x1 80.8 us: shards(): draft_loss = lax.psum(partial_loss, ('grp', 'tp'))]
    reduce_scatter x1 -> x0, waiting for transfers between devices: 77.8 us -> none  [shards(): lax.psum_scatter(jnp.dot(gathered, weight, preferred_element_type=jnp.flo...]
    dot_general x2 -> x0, matrix products: 37.4 us -> none  [the longest x1 18.8 us: shards(): jnp.dot(gathered, weight, preferred_element_type=jnp.float32)]
  transfers between devices with their start and end apart: 3 -> 0, of which waited for: 2 -> 0; matrix products, arithmetic and copies ran while one was open for 0% -> 0% of each run, Pallas kernels for 0% -> 0%
where the time goes in v1:
time: 182 us
  Pallas kernels  173 us (95%)
  local copies, waits for them, and re-layouts  6.2 us (3%)
  between operations  2.4 us (1%)
    pallas_call x1, Pallas kernels, shards(): pl.pallas_call(functools.partial(kernel, cols * lax.axis_size('grp'), spl...  173 us
    unnamed x1, local copies, waits for them, and re-layouts  6.2 us

profile of v1, /device:TPU:1, one launch (start us, length us, event | category | flops | bytes accessed | tf_op | source)
XLA Modules:
  0.0 182.1 jit_solution(2079821424654286027)
XLA Ops:
  0.6 173.5 %shard_map.68 = (bf16[3072,1024]{1,0:T(8,128)(2,1)}, f32[1,1]{1,0:T(1,128)}) custom-call(bf16[256,3072]{1,0:T(8,128)(2,1)} %features.1, bf16[3072,1024]{1,0:T(8,128)(2,1)} %weight.1, f32[1,1024]{1,0:T(1,128)} %bitcast.3, bf16[2048,1024]{1,0:T(8,128)(2,1)} %target.1, s32[256]{0:T(256)} %counts_s.1, s32[2,128]{1,0:T(2,128)} %bitcast.4), custom_call_target="tpu_custom_call" | custom-call | tf_op jit(solution)/shard_map/pallas_call | solution.py:373
  174.1 6.2 %copy.9 = bf16[3072,1024]{1,0:T(8,128)(2,1)} copy(bf16[3072,1024]{1,0:T(8,128)(2,1)} %get-tuple-element.8) | data formatting | bytes 12582912

commit v2 on v1

--- a/solution.py
+++ b/solution.py
@@ -14,15 +14,16 @@
 MESH = pl.DeviceIdType.MESH
 
 TP_OFF = ((0, 1), (0, 3), (0, 2), (1, 0), (1, 1), (1, 3), (1, 2))
+X_OFF = (1, 3, 2)
 GRP_OFF = ((0, 1), (1, 0), (3, 0), (2, 0), (1, 1), (3, 1), (2, 1))
 
 
 def kernel(
     dout, split, features, weight, gain_ref, target, counts_s, counts_v, out, loss_out,
-    fbuf, wbuf, acc, gbuf, stage, hsend, hrecv, hown, hsum, rsrecv, hid, tgt,
+    fbuf, wbuf, acc, gbuf, stage, hsend, hrecv, hown, hsum, xrecv, zsend, zrecv, hid, tgt,
     st_own, st_recv, loss_acc, l1_recv, l2_own, l2_recv,
     w_sem, f_sem, t_sem, o_sem,
-    ag_s, ag_r, hp_s, hp_r, rs_s, rs_r, st_s, st_r, ga_s, ga_r, gp_s, gp_r,
+    ag_s, ag_r, hp_s, hp_r, rx_s, rx_r, rz_s, rz_r, st_s, st_r, gz_s, gz_r, gx_s, gx_r, gp_s, gp_r,
     l1_s, l1_r, l2_s, l2_r,
 ):
     g, t = lax.axis_index("grp"), lax.axis_index("tp")
@@ -33,7 +34,9 @@
     rows_g = features.shape[0]
     n_chunks = len(CHUNKS)
     offs = [sum(CHUNKS[:c]) for c in range(n_chunks)]
-    a_cols, a_half, half = split
+    a_cols, a_low, half = split
+    a_halves = [a_low if c % 2 == 0 else a_cols - a_low for c in range(n_chunks)]
+    place = x * 2 + zh
 
     def grp_dev(dy, dz):
         return lax.rem(y + dy, 4) * 2 + lax.rem(zl + dz, 2)
@@ -46,6 +49,9 @@
     other = t + 1 - 2 * core
 
     tp_peers = [chip(*o) * 2 + core for o in TP_OFF]
+    x_peers, z_peer = tp_peers[:3], tp_peers[3]
+    x_of = [lax.rem(x + dx, 4) for dx in X_OFF]
+    x_from = [lax.rem(x + 4 - dx, 4) for dx in X_OFF]
     grp_peers = [grp_dev(*o) for o in GRP_OFF]
     all_tp = tp_peers + [chip(*o) * 2 + 1 - core for o in TP_OFF] + [other]
 
@@ -84,14 +90,14 @@
 
     def own_rows(c):
         r = CHUNKS[c]
-        return (core * 4 + q // 2) * rows_g + offs[c] + lax.rem(q, 2) * (r // 2)
+        return (core * 4 + x) * rows_g + offs[c] + zh * (r // 2)
 
     t_cps = []
     for c in range(n_chunks):
         r = CHUNKS[c]
         cp = pltpu.make_async_copy(
             target.at[pl.ds(pl.multiple_of(own_rows(c), 16), r // 2), :],
-            tgt.at[pl.ds(4 * 0 + offs[c] // 2, r // 2), :],
+            tgt.at[pl.ds(offs[c] // 2, r // 2), :],
             t_sem.at[c],
         )
         cp.start()
@@ -139,9 +145,9 @@
 
     def round3(c):
         ag_got(c, 4, zym, 0, a_cols)
-        ag_put(c, 8, zym, 0, a_half, yp)
+        ag_put(c, 8, zym, 0, a_halves[c], yp)
         ag_got(c, 5, zyp, 0, a_cols)
-        ag_put(c, 9, zyp, a_half, a_cols - a_half, ym)
+        ag_put(c, 9, zyp, a_halves[c], a_cols - a_halves[c], ym)
 
     def round4(c):
         ag_got(c, 6, yo, 0, half)
@@ -152,12 +158,12 @@
         ag_got(c, 3, zp, a_cols, b_cols)
         ag_got(c, 10, zym, a_cols, b_cols)
         ag_got(c, 11, zyp, a_cols, b_cols)
-        ag_got(c, 8, zyo, 0, a_half)
-        ag_got(c, 9, zyo, a_half, a_cols - a_half)
+        ag_got(c, 8, zyo, 0, a_halves[c])
+        ag_got(c, 9, zyo, a_halves[c], a_cols - a_halves[c])
         ag_got(c, 12, zyo, a_cols, b_cols)
         local[c].wait()
 
-    def matmul_half(c, which, keep):
+    def matmul(c, which, keep, lo, hi):
         r4 = 4 * CHUNKS[c]
         start_row = pl.multiple_of(8 * offs[c] + which * r4, 16)
 
@@ -172,46 +178,69 @@
                 hsend[pl.ds(4 * offs[c], r4), col] = part.astype(jnp.bfloat16)
             return 0
 
-        lax.fori_loop(0, cols // TILE, tile, 0)
-
-    def matmul_other(c):
-        matmul_half(c, 1 - core, False)
+        lax.fori_loop(lo, hi, tile, 0)
+
+    n_cols = cols // TILE
+
+    def matmul_other(c, part):
+        if part == 0:
+            matmul(c, 1 - core, False, 0, n_cols // 2)
+            return
+        matmul(c, 1 - core, False, n_cols // 2, n_cols)
         rows = pl.ds(4 * offs[c], 4 * CHUNKS[c])
         remote(hsend.at[rows, :], hrecv.at[rows, :], hp_s.at[c], hp_r.at[c], (g, other))
 
-    def matmul_mine(c):
-        matmul_half(c, core, True)
-
-    def spread(c):
-        r = CHUNKS[c]
-        base = 4 * offs[c]
+    def matmul_mine(c, part):
+        matmul(c, core, True, part * n_cols // 2, (part + 1) * n_cols // 2)
+
+    def own(c):
+        return pl.ds(offs[c] // 2, CHUNKS[c] // 2)
+
+    def spread_x(c):
+        r = CHUNKS[c]
+        base, n = 4 * offs[c], r // 2
         arrived(hrecv.at[pl.ds(base, 4 * r), :], hp_s.at[c], hp_r.at[c])
 
         def add(i, _):
             lo = pl.multiple_of(i * 16, 16)
             both = hown[pl.ds(lo, 16), :] + hrecv[pl.ds(base + lo, 16), :].astype(jnp.float32)
+            hown[pl.ds(lo, 16), :] = both
             hsum[pl.ds(base + lo, 16), :] = both.astype(jnp.bfloat16)
             return 0
 
         lax.fori_loop(0, 4 * r // 16, add, 0)
-        n = r // 2
-        for k, o in enumerate(TP_OFF):
-            remote(
-                hsum.at[pl.ds(pl.multiple_of(base + chip(*o) * n, 16), n), :],
-                rsrecv.at[k, pl.ds(offs[c] // 2, n), :],
-                rs_s.at[c, k], rs_r.at[c, k], (g, tp_peers[k]),
-            )
+        for j in range(2):
+            for k in range(3):
+                z = 1 - zh if j == 0 else zh
+                remote(
+                    hsum.at[pl.ds(pl.multiple_of(base + (x_of[k] * 2 + z) * n, 16), n), :],
+                    xrecv.at[j, k, own(c), :],
+                    rx_s.at[c, j * 3 + k], rx_r.at[c, j * 3 + k], (g, x_peers[k]),
+                )
+
+    def sum_x(c, j):
+        n = CHUNKS[c] // 2
+        z = 1 - zh if j == 0 else zh
+        for k in range(3):
+            arrived(xrecv.at[j, k, own(c), :], rx_s.at[c, j * 3 + k], rx_r.at[c, j * 3 + k])
+        h = hown[pl.ds(pl.multiple_of((x * 2 + z) * n, 16), n), :]
+        for k in range(3):
+            h = h + xrecv[j, k, own(c), :].astype(jnp.float32)
+        return h
+
+    def spread_z(c):
+        zsend[own(c), :] = sum_x(c, 0).astype(jnp.bfloat16)
+        remote(zsend.at[own(c), :], zrecv.at[own(c), :], rz_s.at[c], rz_r.at[c], (g, z_peer))
+
+    def keep_own(c):
+        hid[own(c), :] = sum_x(c, 1)
 
     def stats(c):
         n = CHUNKS[c] // 2
-        rows = pl.ds(offs[c] // 2, n)
-        mine = pl.multiple_of(q * n, 16)
-        h = hown[pl.ds(mine, n), :]
-        h = h + hrecv[pl.ds(pl.multiple_of(4 * offs[c] + mine, 16), n), :].astype(jnp.float32)
-        for k in range(7):
-            arrived(rsrecv.at[k, rows, :], rs_s.at[c, k], rs_r.at[c, k])
-            h = h + rsrecv[k, rows, :].astype(jnp.float32)
-        hid[pl.ds(0, n), :] = h
+        rows = own(c)
+        arrived(zrecv.at[rows, :], rz_s.at[c], rz_r.at[c])
+        h = hid[rows, :] + zrecv[rows, :].astype(jnp.float32)
+        hid[rows, :] = h
         t_cps[c].wait()
         gh = gain_ref[...] * h
         s1 = jnp.sum(h * h, axis=1, keepdims=True)
@@ -224,9 +253,14 @@
                 st_own.at[rows, :], st_recv.at[k, rows, :], st_s.at[c, k], st_r.at[c, k], (grp_peers[k], t)
             )
 
+    def grad_rows(c, who_core, who_x, who_z):
+        n = CHUNKS[c] // 2
+        lo = 8 * offs[c] + who_core * 4 * CHUNKS[c] + (who_x * 2 + who_z) * n
+        return gbuf.at[pl.ds(pl.multiple_of(lo, 16), n), :]
+
     def gradient(c):
         n = CHUNKS[c] // 2
-        rows = pl.ds(offs[c] // 2, n)
+        rows = own(c)
         total = st_own[rows, :]
         for k in range(7):
             arrived(st_recv.at[k, rows, :], st_s.at[c, k], st_r.at[c, k])
@@ -241,37 +275,46 @@
         )[:, 0:1]
         scale = live / accepted
         gain = gain_ref[...]
-        h = hid[pl.ds(0, n), :]
+        h = hid[rows, :]
         dev = h * inv * gain - tgt[rows, :].astype(jnp.float32)
         res = scale * dev
         coupling = scale * (inv * s2 - s3)
         grad = inv * gain * res - h * (inv * inv * inv * coupling / dout)
-        mine = pl.ds(pl.multiple_of(8 * offs[c] + core * 4 * CHUNKS[c] + q * n, 16), n)
+        mine = pl.ds(pl.multiple_of(8 * offs[c] + core * 4 * CHUNKS[c] + place * n, 16), n)
         gbuf[mine, :] = grad.astype(jnp.bfloat16)
+        ref = gbuf.at[mine, :]
+        remote(ref, ref, gz_s.at[c], gz_r.at[c], (g, z_peer))
+        for k in range(3):
+            remote(ref, ref, gx_s.at[c, k], gx_r.at[c, k], (g, x_peers[k]))
+        remote(ref, ref, gp_s.at[c, 0], gp_r.at[c, 0], (g, other))
         lost = res * dev
         part = loss_acc[...]
         for i in range(n // 8):
             for j in range(cols // 128):
                 part = part + lost[8 * i : 8 * i + 8, 128 * j : 128 * j + 128]
         loss_acc[...] = part
-        for k in range(7):
-            remote(gbuf.at[mine, :], gbuf.at[mine, :], ga_s.at[c, k], ga_r.at[c, k], (g, tp_peers[k]))
-        remote(gbuf.at[mine, :], gbuf.at[mine, :], gp_s.at[c, 7], gp_r.at[c, 7], (g, other))
-
-    def grad_rows(c, who_core, who_chip):
-        n = CHUNKS[c] // 2
-        return gbuf.at[pl.ds(pl.multiple_of(8 * offs[c] + who_core * 4 * CHUNKS[c] + who_chip * n, 16), n), :]
-
-    def pass_on(c):
-        for k, (dz, dx) in enumerate(TP_OFF):
-            ref = grad_rows(c, core, chip((2 - dz) % 2, (4 - dx) % 4))
-            arrived(ref, ga_s.at[c, k], ga_r.at[c, k])
-            remote(ref, ref, gp_s.at[c, k], gp_r.at[c, k], (g, other))
+
+    def pass_x(c):
+        ref = grad_rows(c, core, x, 1 - zh)
+        arrived(ref, gz_s.at[c], gz_r.at[c])
+        for k in range(3):
+            remote(ref, ref, gx_s.at[c, 3 + k], gx_r.at[c, 3 + k], (g, x_peers[k]))
+        remote(ref, ref, gp_s.at[c, 1], gp_r.at[c, 1], (g, other))
+
+    def pass_pair(c):
+        for j in range(2):
+            for k in range(3):
+                ref = grad_rows(c, core, x_from[k], zh if j == 0 else 1 - zh)
+                arrived(ref, gx_s.at[c, j * 3 + k], gx_r.at[c, j * 3 + k])
+                remote(ref, ref, gp_s.at[c, 2 + j * 3 + k], gp_r.at[c, 2 + j * 3 + k], (g, other))
 
     def other_grads(c):
-        arrived(grad_rows(c, 1 - core, q), gp_s.at[c, 7], gp_r.at[c, 7])
-        for k, (dz, dx) in enumerate(TP_OFF):
-            arrived(grad_rows(c, 1 - core, chip((2 - dz) % 2, (4 - dx) % 4)), gp_s.at[c, k], gp_r.at[c, k])
+        arrived(grad_rows(c, 1 - core, x, zh), gp_s.at[c, 0], gp_r.at[c, 0])
+        arrived(grad_rows(c, 1 - core, x, 1 - zh), gp_s.at[c, 1], gp_r.at[c, 1])
+        for j in range(2):
+            for k in range(3):
+                m = 2 + j * 3 + k
+                arrived(grad_rows(c, 1 - core, x_from[k], zh if j == 0 else 1 - zh), gp_s.at[c, m], gp_r.at[c, m])
 
     n_tiles = depth // TILE
     last = n_chunks - 1
@@ -300,42 +343,56 @@
         lax.fori_loop(lo, hi, tile, 0)
 
     loss_acc[...] = jnp.zeros_like(loss_acc)
+    mid = n_tiles // 2
+
+    def do(op, c, *args):
+        if 0 <= c < n_chunks:
+            op(c, *args)
+
+    def outer_first(c):
+        other_grads(c)
+        outer(c, 0, mid)
+
+    def outer_second(c):
+        outer(c, mid, n_tiles)
+
     start(0)
     round1(0)
     round2(0)
-    if n_chunks > 1:
-        start(1)
+    do(start, 1)
     round3(0)
+    do(round1, 1)
     round4(0)
     w_cp.wait()
-    finish(0)
     for c in range(n_chunks):
-        more = c + 1 < n_chunks
-        matmul_other(c)
-        if more:
-            round1(c + 1)
-        matmul_mine(c)
-        if more:
-            round2(c + 1)
-            if c + 2 < n_chunks:
-                start(c + 2)
-        if c > 0:
-            pass_on(c - 1)
-        spread(c)
-        if more:
-            round3(c + 1)
-        if c > 0:
-            other_grads(c - 1)
-            outer(c - 1, 0, n_tiles)
-        if more:
-            round4(c + 1)
-        stats(c)
-        gradient(c)
-        if more:
-            finish(c + 1)
+        finish(c)
+        matmul_other(c, 0)
+        do(stats, c - 1)
+        do(round2, c + 1)
+        do(start, c + 2)
+        matmul_other(c, 1)
+        do(pass_pair, c - 2)
+        matmul_mine(c, 0)
+        do(round3, c + 1)
+        matmul_mine(c, 1)
+        spread_x(c)
+        do(gradient, c - 1)
+        do(round1, c + 2)
+        do(outer_first, c - 2)
+        do(round4, c + 1)
+        spread_z(c)
+        do(pass_x, c - 1)
+        keep_own(c)
+        do(outer_second, c - 2)
+    stats(last)
+    do(pass_pair, last - 1)
+    gradient(last)
     for k, p in enumerate(all_tp):
         remote(loss_acc, l1_recv.at[k], l1_s.at[k], l1_r.at[k], (g, p))
-    pass_on(last)
+    do(outer_first, last - 1)
+    pass_x(last)
+    do(outer_second, last - 1)
+    pass_pair(last)
     sum1 = loss_acc[...]
     for k in range(15):
         arrived(l1_recv.at[k], l1_s.at[k], l1_r.at[k])
@@ -343,8 +400,8 @@
     l2_own[...] = sum1
     for k in range(7):
         remote(l2_own, l2_recv.at[k], l2_s.at[k], l2_r.at[k], (grp_peers[k], t))
-    other_grads(last)
-    outer(last, 0, n_tiles)
+    outer_first(last)
+    outer_second(last)
     sum2 = l2_own[...]
     for k in range(7):
         arrived(l2_recv.at[k], l2_s.at[k], l2_r.at[k])
@@ -368,7 +425,7 @@
     anyspace = pl.BlockSpec(memory_space=pl.ANY)
     vmem = pl.BlockSpec(memory_space=pltpu.VMEM)
     unit = depth // 128
-    a_units = unit * 16 // 24
+    a_units = unit * 15 // 24
     split = (a_units * 128, (a_units // 2) * 128, (unit // 2) * 128)
     out, loss = pl.pallas_call(
         functools.partial(kernel, cols * lax.axis_size("grp"), split),
@@ -388,8 +445,10 @@
             pltpu.VMEM((total // 2, cols), bf),
             pltpu.VMEM((4 * max(CHUNKS), cols), f32),
             pltpu.VMEM((total // 2, cols), bf),
-            pltpu.VMEM((7, own, cols), bf),
-            pltpu.VMEM((max(CHUNKS) // 2, cols), f32),
+            pltpu.VMEM((2, 3, own, cols), bf),
+            pltpu.VMEM((own, cols), bf),
+            pltpu.VMEM((own, cols), bf),
+            pltpu.VMEM((own, cols), f32),
             pltpu.VMEM((own, cols), bf),
             pltpu.VMEM((own, 128), f32),
             pltpu.VMEM((7, own, 128), f32),
@@ -398,8 +457,8 @@
             pltpu.VMEM((8, 128), f32),
             pltpu.VMEM((7, 8, 128), f32),
             dma, dma((n,)), dma((n,)), dma((depth // TILE,)),
-            dma((n, 13)), dma((n, 13)), dma((n,)), dma((n,)), dma((n, 7)), dma((n, 7)),
-            dma((n, 7)), dma((n, 7)), dma((n, 7)), dma((n, 7)), dma((n, 8)), dma((n, 8)),
+            dma((n, 13)), dma((n, 13)), dma((n,)), dma((n,)), dma((n, 6)), dma((n, 6)), dma((n,)), dma((n,)),
+            dma((n, 7)), dma((n, 7)), dma((n,)), dma((n,)), dma((n, 6)), dma((n, 6)), dma((n, 8)), dma((n, 8)),
             dma((15,)), dma((15,)), dma((7,)), dma((7,)),
         ],
         compiler_params=pltpu.CompilerParams(

time: 182 us -> 157 us (0.86)
  Pallas kernels: 173 us -> 149 us
    pallas_call x1, Pallas kernels: 173 us -> 149 us  [shards(): pl.pallas_call(functools.partial(kernel, cols * lax.axis_size('grp'), spl...]
where the time goes in v2:
time: 157 us
  Pallas kernels  149 us (95%)
  local copies, waits for them, and re-layouts  6.2 us (4%)
  between operations  2.4 us (2%)
    pallas_call x1, Pallas kernels, shards(): pl.pallas_call(functools.partial(kernel, cols * lax.axis_size('grp'), spl...  149 us
    unnamed x1, local copies, waits for them, and re-layouts  6.2 us

profile of v2, /device:TPU:1, one launch (start us, length us, event | category | flops | bytes accessed | tf_op | source)
XLA Modules:
  0.0 157.1 jit_solution(4808162440468553429)
XLA Ops:
  0.6 148.5 %shard_map.68 = (bf16[3072,1024]{1,0:T(8,128)(2,1)}, f32[1,1]{1,0:T(1,128)}) custom-call(bf16[256,3072]{1,0:T(8,128)(2,1)} %features.1, bf16[3072,1024]{1,0:T(8,128)(2,1)} %weight.1, f32[1,1024]{1,0:T(1,128)} %bitcast.3, bf16[2048,1024]{1,0:T(8,128)(2,1)} %target.1, s32[256]{0:T(256)} %counts_s.1, s32[2,128]{1,0:T(2,128)} %bitcast.4), custom_call_target="tpu_custom_call" | custom-call | tf_op jit(solution)/shard_map/pallas_call | solution.py:430
  149.1 6.2 %copy.9 = bf16[3072,1024]{1,0:T(8,128)(2,1)} copy(bf16[3072,1024]{1,0:T(8,128)(2,1)} %get-tuple-element.8) | data formatting | bytes 12582912

commit v3 on v2

--- a/solution.py
+++ b/solution.py
@@ -9,7 +9,22 @@
 
 SPEC = 8
 EPS = 1e-06
-CHUNKS = (64, 64, 64, 64)
+CHUNKS = (64, 64, 64, 32, 32)
+ORDER = (
+    ("start", 0, 0), ("r1", 0, 0), ("r2", 0, 0), ("start", 1, 0), ("r3", 0, 0), ("r4", 0, 0), ("r1", 1, 0),
+    ("r2", 1, 0), ("start", 2, 0), ("fin", 0, 0), ("m1", 0, 0), ("m1", 0, 1), ("r3", 1, 0), ("p", 0, 0),
+    ("r4", 1, 0), ("r1", 2, 0), ("q1", 0, 0), ("q2", 0, 0), ("r2", 2, 0), ("start", 3, 0), ("s", 0, 0),
+    ("fin", 1, 0), ("m1", 1, 0), ("m1", 1, 1), ("r3", 2, 0), ("p", 1, 0), ("r1", 3, 0), ("r4", 2, 0),
+    ("q1", 1, 0), ("r2", 3, 0), ("start", 4, 0), ("q2", 1, 0), ("g", 0, 0), ("fin", 2, 0), ("s", 1, 0),
+    ("m1", 2, 0), ("r3", 3, 0), ("m1", 2, 1), ("r4", 3, 0), ("r1", 4, 0), ("x", 0, 0), ("p", 2, 0),
+    ("h", 0, 0), ("r2", 4, 0), ("fin", 3, 0), ("g", 1, 0), ("m1", 3, 0), ("r3", 4, 0), ("q1", 2, 0),
+    ("m1", 3, 1), ("r4", 4, 0), ("h", 1, 0), ("p", 3, 0), ("q2", 2, 0), ("s", 2, 0), ("fin", 4, 0),
+    ("m1", 4, 0), ("x", 0, 1), ("m1", 4, 1), ("g", 2, 0), ("x", 1, 0), ("p", 4, 0), ("d", 0, 0), ("x", 1, 1),
+    ("d", 0, 1), ("h", 2, 0), ("q1", 3, 0), ("q2", 3, 0), ("d", 1, 0), ("x", 2, 0), ("s", 3, 0), ("d", 1, 1),
+    ("q1", 4, 0), ("q2", 4, 0), ("g", 3, 0), ("x", 2, 1), ("s", 4, 0), ("d", 2, 0), ("h", 3, 0), ("x", 3, 0),
+    ("g", 4, 0), ("d", 2, 1), ("x", 3, 1), ("h", 4, 0), ("d", 3, 0), ("x", 4, 0), ("d", 3, 1), ("x", 4, 1),
+    ("d", 4, 0), ("d", 4, 1),
+)
 TILE = 256
 MESH = pl.DeviceIdType.MESH
 
@@ -20,9 +35,9 @@
 
 def kernel(
     dout, split, features, weight, gain_ref, target, counts_s, counts_v, out, loss_out,
-    fbuf, wbuf, acc, gbuf, stage, hsend, hrecv, hown, hsum, xrecv, zsend, zrecv, hid, tgt,
+    fbuf, wbuf, acc, gbuf, hsend, hrecv, hfull, hsum, xrecv, zsend, zrecv, hid, tgt,
     st_own, st_recv, loss_acc, l1_recv, l2_own, l2_recv,
-    w_sem, f_sem, t_sem, o_sem,
+    w_sem, f_sem, t_sem,
     ag_s, ag_r, hp_s, hp_r, rx_s, rx_r, rz_s, rz_r, st_s, st_r, gz_s, gz_r, gx_s, gx_r, gp_s, gp_r,
     l1_s, l1_r, l2_s, l2_r,
 ):
@@ -163,35 +178,30 @@
         ag_got(c, 12, zyo, a_cols, b_cols)
         local[c].wait()
 
-    def matmul(c, which, keep, lo, hi):
-        r4 = 4 * CHUNKS[c]
-        start_row = pl.multiple_of(8 * offs[c] + which * r4, 16)
+    n_cols = cols // TILE
+    parts = 2
+
+    def matmul(c, part):
+        r8 = 8 * CHUNKS[c]
+        rows = pl.ds(8 * offs[c], r8)
 
         def tile(n, _):
             col = pl.ds(pl.multiple_of(n * TILE, TILE), TILE)
-            part = jnp.dot(
-                fbuf[pl.ds(start_row, r4), :], wbuf[:, col], preferred_element_type=jnp.float32
-            )
-            if keep:
-                hown[pl.ds(0, r4), col] = part
-            else:
-                hsend[pl.ds(4 * offs[c], r4), col] = part.astype(jnp.bfloat16)
+            prod = jnp.dot(fbuf[rows, :], wbuf[:, col], preferred_element_type=jnp.float32)
+            hfull[c % 2, pl.ds(0, r8), col] = prod
+            hsend[rows, col] = prod.astype(jnp.bfloat16)
             return 0
 
-        lax.fori_loop(lo, hi, tile, 0)
-
-    n_cols = cols // TILE
-
-    def matmul_other(c, part):
-        if part == 0:
-            matmul(c, 1 - core, False, 0, n_cols // 2)
-            return
-        matmul(c, 1 - core, False, n_cols // 2, n_cols)
-        rows = pl.ds(4 * offs[c], 4 * CHUNKS[c])
-        remote(hsend.at[rows, :], hrecv.at[rows, :], hp_s.at[c], hp_r.at[c], (g, other))
-
-    def matmul_mine(c, part):
-        matmul(c, core, True, part * n_cols // 2, (part + 1) * n_cols // 2)
+        lax.fori_loop(part * n_cols // parts, (part + 1) * n_cols // parts, tile, 0)
+        wide = pl.ds(part * cols // parts, cols // parts)
+        theirs = pl.ds(pl.multiple_of(8 * offs[c] + (1 - core) * (r8 // 2), 16), r8 // 2)
+        remote(
+            hsend.at[theirs, wide], hrecv.at[pl.ds(4 * offs[c], r8 // 2), wide],
+            hp_s.at[c, part], hp_r.at[c, part], (g, other),
+        )
+
+    def mine(c, lo, n):
+        return c % 2, pl.ds(pl.multiple_of(core * 4 * CHUNKS[c] + lo, 16), n)
 
     def own(c):
         return pl.ds(offs[c] // 2, CHUNKS[c] // 2)
@@ -199,12 +209,15 @@
     def spread_x(c):
         r = CHUNKS[c]
         base, n = 4 * offs[c], r // 2
-        arrived(hrecv.at[pl.ds(base, 4 * r), :], hp_s.at[c], hp_r.at[c])
+        for i in range(parts):
+            wide = pl.ds(i * cols // parts, cols // parts)
+            arrived(hrecv.at[pl.ds(base, 4 * r), wide], hp_s.at[c, i], hp_r.at[c, i])
 
         def add(i, _):
             lo = pl.multiple_of(i * 16, 16)
-            both = hown[pl.ds(lo, 16), :] + hrecv[pl.ds(base + lo, 16), :].astype(jnp.float32)
-            hown[pl.ds(lo, 16), :] = both
+            slot, rows = mine(c, lo, 16)
+            both = hfull[slot, rows, :] + hrecv[pl.ds(base + lo, 16), :].astype(jnp.float32)
+            hfull[slot, rows, :] = both
             hsum[pl.ds(base + lo, 16), :] = both.astype(jnp.bfloat16)
             return 0
 
@@ -223,7 +236,8 @@
         z = 1 - zh if j == 0 else zh
         for k in range(3):
             arrived(xrecv.at[j, k, own(c), :], rx_s.at[c, j * 3 + k], rx_r.at[c, j * 3 + k])
-        h = hown[pl.ds(pl.multiple_of((x * 2 + z) * n, 16), n), :]
+        slot, rows = mine(c, (x * 2 + z) * n, n)
+        h = hfull[slot, rows, :]
         for k in range(3):
             h = h + xrecv[j, k, own(c), :].astype(jnp.float32)
         return h
@@ -247,11 +261,11 @@
         s2 = jnp.sum(gh * gh, axis=1, keepdims=True)
         s3 = jnp.sum(gh * tgt[rows, :].astype(jnp.float32), axis=1, keepdims=True)
         lane = lax.broadcasted_iota(jnp.int32, (n, 128), 1)
-        st_own[rows, :] = jnp.where(lane == 0, s1, jnp.where(lane == 1, s2, s3))
+        wide = jnp.where(lane == 0, s1, jnp.where(lane == 1, s2, s3))
+        wide = jnp.concatenate([wide, jnp.zeros((128 - n, 128), jnp.float32)], axis=0)
+        st_own[c] = jnp.transpose(wide)[0:8, :]
         for k in range(7):
-            remote(
-                st_own.at[rows, :], st_recv.at[k, rows, :], st_s.at[c, k], st_r.at[c, k], (grp_peers[k], t)
-            )
+            remote(st_own.at[c], st_recv.at[c, k], st_s.at[c, k], st_r.at[c, k], (grp_peers[k], t))
 
     def grad_rows(c, who_core, who_x, who_z):
         n = CHUNKS[c] // 2
@@ -261,10 +275,12 @@
     def gradient(c):
         n = CHUNKS[c] // 2
         rows = own(c)
-        total = st_own[rows, :]
+        total = st_own[c]
         for k in range(7):
-            arrived(st_recv.at[k, rows, :], st_s.at[c, k], st_r.at[c, k])
-            total = total + st_recv[k, rows, :]
+            arrived(st_recv.at[c, k], st_s.at[c, k], st_r.at[c, k])
+            total = total + st_recv[c, k]
+        total = jnp.concatenate([total, jnp.zeros((120, 128), jnp.float32)], axis=0)
+        total = jnp.transpose(total)[0:n, :]
         s1, s2, s3 = total[:, 0:1], total[:, 1:2], total[:, 2:3]
         inv = lax.rsqrt(s1 / dout + EPS)
         accepted = jnp.sum(counts_v[...].astype(jnp.float32), keepdims=True)
@@ -301,12 +317,11 @@
             remote(ref, ref, gx_s.at[c, 3 + k], gx_r.at[c, 3 + k], (g, x_peers[k]))
         remote(ref, ref, gp_s.at[c, 1], gp_r.at[c, 1], (g, other))
 
-    def pass_pair(c):
-        for j in range(2):
-            for k in range(3):
-                ref = grad_rows(c, core, x_from[k], zh if j == 0 else 1 - zh)
-                arrived(ref, gx_s.at[c, j * 3 + k], gx_r.at[c, j * 3 + k])
-                remote(ref, ref, gp_s.at[c, 2 + j * 3 + k], gp_r.at[c, 2 + j * 3 + k], (g, other))
+    def pass_pair(c, j):
+        for k in range(3):
+            ref = grad_rows(c, core, x_from[k], zh if j == 0 else 1 - zh)
+            arrived(ref, gx_s.at[c, j * 3 + k], gx_r.at[c, j * 3 + k])
+            remote(ref, ref, gp_s.at[c, 2 + j * 3 + k], gp_r.at[c, 2 + j * 3 + k], (g, other))
 
     def other_grads(c):
         arrived(grad_rows(c, 1 - core, x, zh), gp_s.at[c, 0], gp_r.at[c, 0])
@@ -319,97 +334,64 @@
     n_tiles = depth // TILE
     last = n_chunks - 1
 
-    def outer(c, lo, hi):
+    def outer(c, part):
+        if part == 0:
+            other_grads(c)
         rows = pl.ds(8 * offs[c], 8 * CHUNKS[c])
 
         def tile(i, _):
             k = pl.ds(pl.multiple_of(i * TILE, TILE), TILE)
-            for n in range(cols // TILE):
+            for n in range(n_cols):
                 col = pl.ds(n * TILE, TILE)
-                part = lax.dot_general(
+                prod = lax.dot_general(
                     fbuf[rows, k], gbuf[rows, col], (((0,), (0,)), ((), ())),
                     preferred_element_type=jnp.float32,
                 )
                 if c > 0:
-                    part = part + acc[k, col]
+                    prod = prod + acc[k, col]
                 if c == last:
-                    stage[k, col] = part.astype(jnp.bfloat16)
+                    out[k, col] = prod.astype(jnp.bfloat16)
                 else:
-                    acc[k, col] = part
-            if c == last:
-                pltpu.make_async_copy(stage.at[k, :], out.at[k, :], o_sem.at[i]).start()
+                    acc[k, col] = prod
             return 0
 
-        lax.fori_loop(lo, hi, tile, 0)
+        lax.fori_loop(part * n_tiles // 2, (part + 1) * n_tiles // 2, tile, 0)
+
+    def share_loss():
+        for k, p in enumerate(all_tp):
+            remote(loss_acc, l1_recv.at[k], l1_s.at[k], l1_r.at[k], (g, p))
+
+    def pass_loss():
+        total = loss_acc[...]
+        for k in range(15):
+            arrived(l1_recv.at[k], l1_s.at[k], l1_r.at[k])
+            total = total + l1_recv[k]
+        l2_own[...] = total
+        for k in range(7):
+            remote(l2_own, l2_recv.at[k], l2_s.at[k], l2_r.at[k], (grp_peers[k], t))
 
     loss_acc[...] = jnp.zeros_like(loss_acc)
-    mid = n_tiles // 2
-
-    def do(op, c, *args):
-        if 0 <= c < n_chunks:
-            op(c, *args)
-
-    def outer_first(c):
-        other_grads(c)
-        outer(c, 0, mid)
-
-    def outer_second(c):
-        outer(c, mid, n_tiles)
-
-    start(0)
-    round1(0)
-    round2(0)
-    do(start, 1)
-    round3(0)
-    do(round1, 1)
-    round4(0)
-    w_cp.wait()
-    for c in range(n_chunks):
-        finish(c)
-        matmul_other(c, 0)
-        do(stats, c - 1)
-        do(round2, c + 1)
-        do(start, c + 2)
-        matmul_other(c, 1)
-        do(pass_pair, c - 2)
-        matmul_mine(c, 0)
-        do(round3, c + 1)
-        matmul_mine(c, 1)
-        spread_x(c)
-        do(gradient, c - 1)
-        do(round1, c + 2)
-        do(outer_first, c - 2)
-        do(round4, c + 1)
-        spread_z(c)
-        do(pass_x, c - 1)
-        keep_own(c)
-        do(outer_second, c - 2)
-    stats(last)
-    do(pass_pair, last - 1)
-    gradient(last)
-    for k, p in enumerate(all_tp):
-        remote(loss_acc, l1_recv.at[k], l1_s.at[k], l1_r.at[k], (g, p))
-    do(outer_first, last - 1)
-    pass_x(last)
-    do(outer_second, last - 1)
-    pass_pair(last)
-    sum1 = loss_acc[...]
-    for k in range(15):
-        arrived(l1_recv.at[k], l1_s.at[k], l1_r.at[k])
-        sum1 = sum1 + l1_recv[k]
-    l2_own[...] = sum1
-    for k in range(7):
-        remote(l2_own, l2_recv.at[k], l2_s.at[k], l2_r.at[k], (grp_peers[k], t))
-    outer_first(last)
-    outer_second(last)
+    steps = {
+        "start": start, "r1": round1, "r2": round2, "r3": round3, "r4": round4, "fin": finish,
+        "p": spread_x, "q1": spread_z, "q2": keep_own, "s": stats, "g": gradient, "h": pass_x,
+    }
+    parted = {"m1": matmul, "x": pass_pair, "d": outer}
+    for step, c, part in ORDER:
+        if (step, c, part) == ("m1", 0, 0):
+            w_cp.wait()
+        if (step, c, part) == ("d", last, 0):
+            pass_loss()
+        if step in parted:
+            parted[step](c, part)
+        else:
+            steps[step](c)
+        if (step, c) == ("g", last):
+            share_loss()
     sum2 = l2_own[...]
     for k in range(7):
         arrived(l2_recv.at[k], l2_s.at[k], l2_r.at[k])
         sum2 = sum2 + l2_recv[k]
     loss_out[0, 0] = 0.5 * jnp.sum(sum2)
-    for i in range(n_tiles):
-        k = pl.ds(i * TILE, TILE)
-        pltpu.make_async_copy(stage.at[k, :], out.at[k, :], o_sem.at[i]).wait()
     for cp in sends:
         cp.wait_send()
 
@@ -430,39 +412,38 @@
     out, loss = pl.pallas_call(
         functools.partial(kernel, cols * lax.axis_size("grp"), split),
         out_shape=(
-            jax.ShapeDtypeStruct((depth, cols), bf),
+            pltpu.VMEM((depth, cols), bf),
             jax.ShapeDtypeStruct((1, 1), f32),
         ),
         in_specs=[anyspace, anyspace, vmem, anyspace, pl.BlockSpec(memory_space=pltpu.SMEM), vmem],
-        out_specs=(anyspace, pl.BlockSpec(memory_space=pltpu.SMEM)),
+        out_specs=(vmem, pl.BlockSpec(memory_space=pltpu.SMEM)),
         scratch_shapes=[
             pltpu.VMEM((total, depth), bf),
             pltpu.VMEM((depth, cols), bf),
             pltpu.VMEM((depth, cols), f32),
             pltpu.VMEM((total, cols), bf),
-            pltpu.VMEM((depth, cols), bf),
+            pltpu.VMEM((total, cols), bf),
             pltpu.VMEM((total // 2, cols), bf),
-            pltpu.VMEM((total // 2, cols), bf),
-            pltpu.VMEM((4 * max(CHUNKS), cols), f32),
+            pltpu.VMEM((2, 8 * max(CHUNKS), cols), f32),
             pltpu.VMEM((total // 2, cols), bf),
             pltpu.VMEM((2, 3, own, cols), bf),
             pltpu.VMEM((own, cols), bf),
             pltpu.VMEM((own, cols), bf),
             pltpu.VMEM((own, cols), f32),
             pltpu.VMEM((own, cols), bf),
-            pltpu.VMEM((own, 128), f32),
-            pltpu.VMEM((7, own, 128), f32),
+            pltpu.VMEM((n, 8, 128), f32),
+            pltpu.VMEM((n, 7, 8, 128), f32),
             pltpu.VMEM((8, 128), f32),
             pltpu.VMEM((15, 8, 128), f32),
             pltpu.VMEM((8, 128), f32),
             pltpu.VMEM((7, 8, 128), f32),
-            dma, dma((n,)), dma((n,)), dma((depth // TILE,)),
-            dma((n, 13)), dma((n, 13)), dma((n,)), dma((n,)), dma((n, 6)), dma((n, 6)), dma((n,)), dma((n,)),
+            dma, dma((n,)), dma((n,)),
+            dma((n, 13)), dma((n, 13)), dma((n, 2)), dma((n, 2)), dma((n, 6)), dma((n, 6)), dma((n,)), dma((n,)),
             dma((n, 7)), dma((n, 7)), dma((n,)), dma((n,)), dma((n, 6)), dma((n, 6)), dma((n, 8)), dma((n, 8)),
             dma((15,)), dma((15,)), dma((7,)), dma((7,)),
         ],
         compiler_params=pltpu.CompilerParams(
-            collective_id=0, has_side_effects=True, vmem_limit_bytes=64 * 1024 * 1024 - 65536
+            collective_id=0, has_side_effects=True, vmem_limit_bytes=54 * 1024 * 1024
         ),
     )(features, weight, norm_gain.reshape(1, cols), target, counts, counts.reshape(2, -1))
     return out, loss[0, 0]

time: 157 us -> 147 us (0.936)
  Pallas kernels: 149 us -> 142 us
  local copies, waits for them, and re-layouts: 6.2 us -> 2.71 us
    pallas_call x1, Pallas kernels: 149 us -> 142 us  [shards(): pl.pallas_call(functools.partial(kernel, cols * lax.axis_size('grp'), spl...]
    unnamed x1, local copies, waits for them, and re-layouts: 6.2 us -> 2.71 us
where the time goes in v3:
time: 147 us
  Pallas kernels  142 us (97%)
  local copies, waits for them, and re-layouts  2.71 us (2%)
  between operations  2.33 us (2%)
    pallas_call x1, Pallas kernels, shards(): pl.pallas_call(functools.partial(kernel, cols * lax.axis_size('grp'), spl...  142 us

profile of v3, /device:TPU:1, one launch (start us, length us, event | category | flops | bytes accessed | tf_op | source)
XLA Modules:
  0.0 147.1 jit_solution(14474689300483989085)
XLA Ops:
  0.6 142.0 %shard_map.68 = (bf16[3072,1024]{1,0:T(8,128)(2,1)S(1)}, f32[1,1]{1,0:T(1,128)}) custom-call(bf16[256,3072]{1,0:T(8,128)(2,1)} %features.1, bf16[3072,1024]{1,0:T(8,128)(2,1)} %weight.1, f32[1,1024]{1,0:T(1,128)} %bitcast.3, bf16[2048,1024]{1,0:T(8,128)(2,1)} %target.1, s32[256]{0:T(256)} %counts_s.1, s32[2,128]{1,0:T(2,128)} %bitcast.4), custom_call_target="tpu_custom_call" | custom-call | tf_op jit(solution)/shard_map/pallas_call | solution.py:412
  142.7 2.7 %copy.9 = bf16[3072,1024]{1,0:T(8,128)(2,1)} copy(bf16[3072,1024]{1,0:T(8,128)(2,1)S(1)} %get-tuple-element.6) | data formatting | bytes 12582912

commit v4 on v3

v4 whole, which is shorter than its diff:
```python
import functools

import jax
import jax.numpy as jnp
from jax import lax
from jax.experimental import pallas as pl
from jax.experimental.pallas import tpu as pltpu
from jax.sharding import PartitionSpec as P

SPEC = 8
EPS = 1e-06
CHUNKS = (32, 32, 32, 32, 32, 32, 32, 32)
GROUPS = ((0, 1), (2, 3), (4, 5), (6,), (7,))
ORDER = (
    ("za", 0, 0), ("o1", 0, 0), ("o2", 0, 0), ("zb", 0, 0), ("za", 1, 0), ("o1", 1, 0), ("r2", 0, 0),
    ("r1", 0, 0), ("zb", 1, 0), ("r5", 0, 0), ("r2", 1, 0), ("r1", 1, 0), ("r4", 0, 0), ("za", 2, 0),
    ("r3", 0, 0), ("zb", 2, 0), ("r4", 1, 0), ("o2", 1, 0), ("r3", 1, 0), ("r1", 2, 0), ("za", 3, 0),
    ("fin", 0, 0), ("m1", 0, 0), ("m1", 0, 1), ("r5", 1, 0), ("o1", 2, 0), ("p", 0, 0), ("r1", 3, 0),
    ("zb", 3, 0), ("r3", 2, 0), ("za", 4, 0), ("r2", 2, 0), ("q1", 0, 0), ("fin", 1, 0), ("m1", 1, 0),
    ("r3", 3, 0), ("zb", 4, 0), ("q2", 0, 0), ("m1", 1, 1), ("o2", 2, 0), ("za", 5, 0), ("r1", 4, 0),
    ("p", 1, 0), ("r4", 2, 0), ("s", 0, 0), ("o1", 3, 0), ("zb", 5, 0), ("r5", 2, 0), ("q1", 1, 0),
    ("r1", 5, 0), ("q2", 1, 0), ("r3", 4, 0), ("g", 0, 0), ("r2", 3, 0), ("za", 6, 0), ("r3", 5, 0),
    ("fin", 2, 0), ("x", 0, 0), ("o2", 3, 0), ("zb", 6, 0), ("m1", 2, 0), ("s", 1, 0), ("r4", 3, 0),
    ("h", 0, 0), ("m1", 2, 1), ("r1", 6, 0), ("za", 7, 0), ("p", 2, 0), ("r5", 3, 0), ("o1", 4, 0),
    ("x", 0, 1), ("o2", 4, 0), ("g", 1, 0), ("r3", 6, 0), ("q1", 2, 0), ("r1", 7, 0), ("r2", 4, 0),
    ("q2", 2, 0), ("zb", 7, 0), ("x", 1, 0), ("r5", 4, 0), ("fin", 3, 0), ("m1", 3, 0), ("o1", 5, 0),
    ("h", 1, 0), ("m1", 3, 1), ("r3", 7, 0), ("s", 2, 0), ("p", 3, 0), ("r4", 4, 0), ("o2", 5, 0), ("x", 1, 1),
    ("r2", 5, 0), ("fin", 4, 0), ("q1", 3, 0), ("m1", 4, 0), ("r5", 5, 0), ("o1", 6, 0), ("g", 2, 0),
    ("q2", 3, 0), ("m1", 4, 1), ("r4", 5, 0), ("o2", 6, 0), ("s", 3, 0), ("d", 0, 0), ("o1", 7, 0),
    ("r2", 6, 0), ("x", 2, 0), ("p", 4, 0), ("d", 0, 1), ("r5", 6, 0), ("h", 2, 0), ("d", 0, 2), ("o2", 7, 0),
    ("fin", 5, 0), ("m1", 5, 0), ("r2", 7, 0), ("g", 3, 0), ("q1", 4, 0), ("q2", 4, 0), ("m1", 5, 1),
    ("r4", 6, 0), ("x", 2, 1), ("d", 0, 3), ("r5", 7, 0), ("h", 3, 0), ("x", 3, 0), ("p", 5, 0), ("s", 4, 0),
    ("r4", 7, 0), ("fin", 6, 0), ("m1", 6, 0), ("x", 3, 1), ("m1", 6, 1), ("q1", 5, 0), ("p", 6, 0),
    ("g", 4, 0), ("q2", 5, 0), ("fin", 7, 0), ("m1", 7, 0), ("s", 5, 0), ("m1", 7, 1), ("h", 4, 0),
    ("q1", 6, 0), ("d", 1, 0), ("p", 7, 0), ("x", 4, 0), ("g", 5, 0), ("q2", 6, 0), ("s", 6, 0), ("d", 1, 1),
    ("x", 4, 1), ("d", 1, 2), ("h", 5, 0), ("q1", 7, 0), ("d", 1, 3), ("g", 6, 0), ("q2", 7, 0), ("x", 5, 0),
    ("s", 7, 0), ("x", 5, 1), ("h", 6, 0), ("x", 6, 0), ("g", 7, 0), ("d", 2, 0), ("x", 6, 1), ("d", 2, 1),
    ("h", 7, 0), ("d", 2, 2), ("x", 7, 0), ("d", 2, 3), ("d", 3, 0), ("x", 7, 1), ("d", 3, 1), ("d", 3, 2),
    ("d", 3, 3), ("d", 4, 0), ("d", 4, 1), ("d", 4, 2), ("d", 4, 3),
)
TILE = 256
RING = 64
AG_SEM = (0, 1, 2, 3, 4, 5, 6, 7, 8, 8, 3, 3, 3, 9, 10)
MESH = pl.DeviceIdType.MESH

TP_OFF = ((0, 1), (0, 3), (0, 2), (1, 0), (1, 1), (1, 3), (1, 2))
X_OFF = (1, 3, 2)
GRP_OFF = ((0, 1), (1, 0), (3, 0), (2, 0), (1, 1), (3, 1), (2, 1))


def kernel(
    dout, split, features, weight, gain_ref, target, counts_s, counts_v, out, loss_out,
    fbuf, wbuf, acc, gbuf, hsend, hrecv, hfull, hsum, xrecv, zsend, zrecv, hid, tgt,
    st_own, st_recv, loss_acc, l1_recv, l2_own, l2_recv,
    w_sem, f_sem, t_sem, send_sem,
    ag_r, hp_r, rx_r, rz_r, st_r, gz_r, gx_r, gp_r,
    l1_r, l2_r,
):
    g, t = lax.axis_index("grp"), lax.axis_index("tp")
    y, zl = g // 2, lax.rem(g, 2)
    core, q = lax.rem(t, 2), t // 2
    zh, x = q // 4, lax.rem(q, 4)
    depth, cols = wbuf.shape
    rows_g = features.shape[0]
    n_chunks = len(CHUNKS)
    offs = [sum(CHUNKS[:c]) for c in range(n_chunks)]
    a_cols, a_low, half = split
    a_halves = [a_low if c % 2 == 0 else a_cols - a_low for c in range(n_chunks)]
    place = x * 2 + zh

    def grp_dev(dy, dz):
        return lax.rem(y + dy, 4) * 2 + lax.rem(zl + dz, 2)

    def chip(dz, dx):
        return lax.rem(zh + dz, 2) * 4 + lax.rem(x + dx, 4)

    zp, yp, ym, yo = grp_dev(0, 1), grp_dev(1, 0), grp_dev(3, 0), grp_dev(2, 0)
    zyp, zym, zyo = grp_dev(1, 1), grp_dev(3, 1), grp_dev(2, 1)
    other = t + 1 - 2 * core

    tp_peers = [chip(*o) * 2 + core for o in TP_OFF]
    x_peers, z_peer = tp_peers[:3], tp_peers[3]
    x_of = [lax.rem(x + dx, 4) for dx in X_OFF]
    x_from = [lax.rem(x + 4 - dx, 4) for dx in X_OFF]
    grp_peers = [grp_dev(*o) for o in GRP_OFF]
    all_tp = tp_peers + [chip(*o) * 2 + 1 - core for o in TP_OFF] + [other]

    barrier = pltpu.get_barrier_semaphore()
    for p in grp_peers:
        pl.semaphore_signal(barrier, inc=1, device_id=(p, t), device_id_type=MESH)
    for p in all_tp:
        pl.semaphore_signal(barrier, inc=1, device_id=(g, p), device_id_type=MESH)

    sends = []

    sent = [0]

    def remote(src, dst, rsem, dev):
        if len(sends) == RING:
            sends.pop(0).wait_send()
        cp = pltpu.make_async_remote_copy(
            src_ref=src, dst_ref=dst, send_sem=send_sem.at[sent[0] % RING], recv_sem=rsem,
            device_id=dev, device_id_type=MESH,
        )
        cp.start()
        sends.append(cp)
        sent[0] += 1

    def arrived(dst, rsem):
        pltpu.make_async_remote_copy(
            src_ref=dst, dst_ref=dst, send_sem=send_sem.at[0], recv_sem=rsem,
            device_id=(zp, t), device_id_type=MESH,
        ).wait_recv()

    def slot_of(who):
        return lax.rem(who, 2) * 4 + who // 2

    local = []
    for c in range(n_chunks):
        r = CHUNKS[c]
        cp = pltpu.make_async_copy(
            features.at[pl.ds(offs[c], r), :],
            fbuf.at[pl.ds(pl.multiple_of(8 * offs[c] + slot_of(g) * r, 16), r), :],
            f_sem.at[c],
        )
        cp.start()
        local.append(cp)
    w_cp = pltpu.make_async_copy(weight, wbuf, w_sem)
    w_cp.start()

    def own_rows(c):
        r = CHUNKS[c]
        return (x * 2 + core) * rows_g + offs[c] + zh * (r // 2)

    t_cps = []
    for c in range(n_chunks):
        r = CHUNKS[c]
        cp = pltpu.make_async_copy(
            target.at[pl.ds(pl.multiple_of(own_rows(c), 16), r // 2), :],
            tgt.at[pl.ds(offs[c] // 2, r // 2), :],
            t_sem.at[c],
        )
        cp.start()
        t_cps.append(cp)

    pl.semaphore_wait(barrier, len(grp_peers) + len(all_tp))

    def seg(c, who, lo, n):
        r = CHUNKS[c]
        return fbuf.at[pl.ds(pl.multiple_of(8 * offs[c] + slot_of(who) * r, 16), r), pl.ds(lo, n)]

    def ag_put(c, k, who, lo, n, dev):
        remote(seg(c, who, lo, n), seg(c, who, lo, n), ag_r.at[c, AG_SEM[k]], (dev, t))

    def ag_own(c, k, lo, n, dev):
        r = CHUNKS[c]
        remote(
            features.at[pl.ds(offs[c], r), pl.ds(lo, n)], seg(c, g, lo, n),
            ag_r.at[c, AG_SEM[k]], (dev, t),
        )

    def ag_got(c, k, who, lo, n):
        arrived(seg(c, who, lo, n), ag_r.at[c, AG_SEM[k]])

    b_cols = depth - a_cols

    rest = depth - half

    def own_z_first(c):
        ag_own(c, 0, 0, a_cols, zp)

    def own_z_second(c):
        ag_own(c, 3, a_cols, b_cols, zp)

    def own_y_first(c):
        ag_own(c, 1, 0, half, yp)
        ag_own(c, 2, half, rest, ym)

    def own_y_second(c):
        ag_own(c, 13, half, rest, yp)
        ag_own(c, 14, 0, half, ym)

    def round1(c):
        ag_got(c, 0, zp, 0, a_cols)
        ag_put(c, 4, zp, 0, a_cols, yp)
        ag_put(c, 5, zp, 0, a_cols, ym)

    def round2(c):
        ag_got(c, 1, ym, 0, half)
        ag_put(c, 6, ym, 0, half, yp)
        ag_got(c, 2, yp, half, rest)
        ag_put(c, 7, yp, half, rest, ym)

    def round3(c):
        ag_got(c, 4, zym, 0, a_cols)
        ag_put(c, 8, zym, 0, a_halves[c], yp)
        ag_got(c, 5, zyp, 0, a_cols)
        ag_put(c, 9, zyp, a_halves[c], a_cols - a_halves[c], ym)

    def round4(c):
        ag_got(c, 7, yo, half, rest)
        ag_put(c, 12, yo, a_cols, b_cols, zp)

    def round5(c):
        ag_got(c, 13, ym, half, rest)
        ag_put(c, 10, ym, a_cols, b_cols, zp)
        ag_put(c, 11, yp, a_cols, b_cols, zp)

    def finish(c):
        r = CHUNKS[c]
        ag_got(c, 6, yo, 0, half)
        ag_got(c, 14, yp, 0, half)
        ag_got(c, 8, zyo, 0, a_cols)
        plane = pl.ds(pl.multiple_of(8 * offs[c] + (1 - zl) * 4 * r, 16), 4 * r)
        arrived(fbuf.at[plane, pl.ds(a_cols, b_cols)], ag_r.at[c, AG_SEM[3]])
        local[c].wait()

    n_cols = cols // TILE
    parts = 2

    def matmul(c, part):
        r8 = 8 * CHUNKS[c]
        rows = pl.ds(8 * offs[c], r8)

        def tile(n, _):
            col = pl.ds(pl.multiple_of(n * TILE, TILE), TILE)
            prod = jnp.dot(fbuf[rows, :], wbuf[:, col], preferred_element_type=jnp.float32)
            hfull[c % 2, pl.ds(0, r8), col] = prod
            hsend[rows, col] = prod.astype(jnp.bfloat16)
            return 0

        lax.fori_loop(part * n_cols // parts, (part + 1) * n_cols // parts, tile, 0)
        wide = pl.ds(part * cols // parts, cols // parts)
        theirs = pl.ds(pl.multiple_of(8 * offs[c] + (1 - core) * (r8 // 2), 16), r8 // 2)
        remote(
            hsend.at[theirs, wide], hrecv.at[pl.ds(4 * offs[c], r8 // 2), wide],
            hp_r.at[c, part], (g, other),
        )

    def mine(c, lo, n):
        return c % 2, pl.ds(pl.multiple_of(core * 4 * CHUNKS[c] + lo, 16), n)

    def own(c):
        return pl.ds(offs[c] // 2, CHUNKS[c] // 2)

    def spread_x(c):
        r = CHUNKS[c]
        base, n = 4 * offs[c], r // 2
        for i in range(parts):
            wide = pl.ds(i * cols // parts, cols // parts)
            arrived(hrecv.at[pl.ds(base, 4 * r), wide], hp_r.at[c, i])

        def add(i, _):
            lo = pl.multiple_of(i * 16, 16)
            slot, rows = mine(c, lo, 16)
            both = hfull[slot, rows, :] + hrecv[pl.ds(base + lo, 16), :].astype(jnp.float32)
            hfull[slot, rows, :] = both
            hsum[pl.ds(base + lo, 16), :] = both.astype(jnp.bfloat16)
            return 0

        lax.fori_loop(0, 4 * r // 16, add, 0)
        for j in range(2):
            for k in range(3):
                z = 1 - zh if j == 0 else zh
                remote(
                    hsum.at[pl.ds(pl.multiple_of(base + (x_of[k] * 2 + z) * n, 16), n), :],
                    xrecv.at[j, k, own(c), :],
                    rx_r.at[c, j], (g, x_peers[k]),
                )

    def sum_x(c, j):
        n = CHUNKS[c] // 2
        z = 1 - zh if j == 0 else zh
        arrived(xrecv.at[j, :, own(c), :], rx_r.at[c, j])
        slot, rows = mine(c, (x * 2 + z) * n, n)
        h = hfull[slot, rows, :]
        for k in range(3):
            h = h + xrecv[j, k, own(c), :].astype(jnp.float32)
        return h

    def spread_z(c):
        zsend[own(c), :] = sum_x(c, 0).astype(jnp.bfloat16)
        remote(zsend.at[own(c), :], zrecv.at[own(c), :], rz_r.at[c], (g, z_peer))

    def keep_own(c):
        hid[own(c), :] = sum_x(c, 1)

    def stats(c):
        n = CHUNKS[c] // 2
        rows = own(c)
        arrived(zrecv.at[rows, :], rz_r.at[c])
        h = hid[rows, :] + zrecv[rows, :].astype(jnp.float32)
        hid[rows, :] = h
        t_cps[c].wait()
        gh = gain_ref[...] * h
        s1 = jnp.sum(h * h, axis=1, keepdims=True)
        s2 = jnp.sum(gh * gh, axis=1, keepdims=True)
        s3 = jnp.sum(gh * tgt[rows, :].astype(jnp.float32), axis=1, keepdims=True)
        lane = lax.broadcasted_iota(jnp.int32, (n, 128), 1)
        wide = jnp.where(lane == 0, s1, jnp.where(lane == 1, s2, s3))
        wide = jnp.concatenate([wide, jnp.zeros((128 - n, 128), jnp.float32)], axis=0)
        st_own[c] = jnp.transpose(wide)[0:8, :]
        for k in range(7):
            remote(st_own.at[c], st_recv.at[c, k], st_r.at[c], (grp_peers[k], t))

    def grad_rows(c, who_core, who_x, who_z):
        n = CHUNKS[c] // 2
        lo = 8 * offs[c] + who_core * 4 * CHUNKS[c] + (who_x * 2 + who_z) * n
        return gbuf.at[pl.ds(pl.multiple_of(lo, 16), n), :]

    def gradient(c):
        n = CHUNKS[c] // 2
        rows = own(c)
        total = st_own[c]
        arrived(st_recv.at[c], st_r.at[c])
        for k in range(7):
            total = total + st_recv[c, k]
        total = jnp.concatenate([total, jnp.zeros((120, 128), jnp.float32)], axis=0)
        total = jnp.transpose(total)[0:n, :]
        s1, s2, s3 = total[:, 0:1], total[:, 1:2], total[:, 2:3]
        inv = lax.rsqrt(s1 / dout + EPS)
        accepted = jnp.sum(counts_v[...].astype(jnp.float32), keepdims=True)
        first = own_rows(c) // SPEC
        sub = lax.broadcasted_iota(jnp.int32, (SPEC, 128), 0)
        live = jnp.concatenate(
            [(sub < counts_s[first + i]).astype(jnp.float32) for i in range(n // SPEC)], axis=0
        )[:, 0:1]
        scale = live / accepted
        gain = gain_ref[...]
        h = hid[rows, :]
        dev = h * inv * gain - tgt[rows, :].astype(jnp.float32)
        res = scale * dev
        coupling = scale * (inv * s2 - s3)
        grad = inv * gain * res - h * (inv * inv * inv * coupling / dout)
        mine = pl.ds(pl.multiple_of(8 * offs[c] + core * 4 * CHUNKS[c] + place * n, 16), n)
        gbuf[mine, :] = grad.astype(jnp.bfloat16)
        ref = gbuf.at[mine, :]
        remote(ref, ref, gz_r.at[c], (g, z_peer))
        for k in range(3):
            remote(ref, ref, gx_r.at[c, k], (g, x_peers[k]))
        remote(ref, ref, gp_r.at[c], (g, other))
        lost = res * dev
        part = loss_acc[...]
        for i in range(n // 8):
            for j in range(cols // 128):
                part = part + lost[8 * i : 8 * i + 8, 128 * j : 128 * j + 128]
        loss_acc[...] = part

    def pass_x(c):
        ref = grad_rows(c, core, x, 1 - zh)
        arrived(ref, gz_r.at[c])
        for k in range(3):
            remote(ref, ref, gx_r.at[c, 3 + k], (g, x_peers[k]))
        remote(ref, ref, gp_r.at[c], (g, other))

    def pass_pair(c, j):
        for k in range(3):
            ref = grad_rows(c, core, x_from[k], zh if j == 0 else 1 - zh)
            arrived(ref, gx_r.at[c, j * 3 + k])
            remote(ref, ref, gp_r.at[c], (g, other))

    def other_grads(c):
        r4 = 4 * CHUNKS[c]
        arrived(gbuf.at[pl.ds(pl.multiple_of(8 * offs[c] + (1 - core) * r4, 16), r4), :], gp_r.at[c])

    n_tiles = depth // TILE
    last = n_chunks - 1

    def outer(i, part):
        if part == 0:
            for c in GROUPS[i]:
                other_grads(c)
        rows = pl.ds(8 * offs[GROUPS[i][0]], 8 * sum(CHUNKS[c] for c in GROUPS[i]))

        def tile(j, _):
            k = pl.ds(pl.multiple_of(j * TILE, TILE), TILE)
            turned = jnp.transpose(fbuf[rows, k])
            for n in range(n_cols):
                col = pl.ds(n * TILE, TILE)
                prod = jnp.dot(turned, gbuf[rows, col], preferred_element_type=jnp.float32)
                if i > 0:
                    prod = prod + acc[k, col]
                if i == len(GROUPS) - 1:
                    out[k, col] = prod.astype(jnp.bfloat16)
                else:
                    acc[k, col] = prod
            return 0

        lax.fori_loop(part * n_tiles // 4, (part + 1) * n_tiles // 4, tile, 0)

    def share_loss():
        for k, p in enumerate(all_tp):
            remote(loss_acc, l1_recv.at[k], l1_r, (g, p))

    def pass_loss():
        total = loss_acc[...]
        arrived(l1_recv, l1_r)
        for k in range(15):
            total = total + l1_recv[k]
        l2_own[...] = total
        for k in range(7):
            remote(l2_own, l2_recv.at[k], l2_r, (grp_peers[k], t))

    loss_acc[...] = jnp.zeros_like(loss_acc)
    steps = {
        "za": own_z_first, "zb": own_z_second, "o1": own_y_first, "o2": own_y_second,
        "r1": round1, "r2": round2, "r3": round3, "r4": round4, "r5": round5, "fin": finish,
        "p": spread_x, "q1": spread_z, "q2": keep_own, "s": stats, "g": gradient, "h": pass_x,
    }
    parted = {"m1": matmul, "x": pass_pair, "d": outer}
    gathering = True
    for step, c, part in ORDER:
        if (step, c, part) == ("m1", 0, 0):
            w_cp.wait()
        if step in parted:
            parted[step](c, part)
        else:
            steps[step](c)
        if (step, c) == ("g", last):
            share_loss()
        if (step, c, part) == ("x", last, 0):
            pass_loss()
        if (step, c) == ("fin", last):
            gathering = False
        for _ in range(4 if gathering else 2):
            if len(sends) > (50 if gathering else 24):
                sends.pop(0).wait_send()
    sum2 = l2_own[...]
    arrived(l2_recv, l2_r)
    for k in range(7):
        sum2 = sum2 + l2_recv[k]
    loss_out[0, 0] = 0.5 * jnp.sum(sum2)
    for cp in sends:
        cp.wait_send()


def shards(features, weight, norm_gain, target, counts):
    rows_g, depth = features.shape
    cols = weight.shape[1]
    total = target.shape[0]
    n = len(CHUNKS)
    bf, f32 = jnp.bfloat16, jnp.float32
    own = total // 16
    dma = pltpu.SemaphoreType.DMA
    anyspace = pl.BlockSpec(memory_space=pl.ANY)
    vmem = pl.BlockSpec(memory_space=pltpu.VMEM)
    unit = depth // 128
    a_units = unit * 14 // 24
    split = (a_units * 128, (a_units // 2) * 128, (unit // 2) * 128)
    out, loss = pl.pallas_call(
        functools.partial(kernel, cols * lax.axis_size("grp"), split),
        out_shape=(
            pltpu.VMEM((depth, cols), bf),
            jax.ShapeDtypeStruct((1, 1), f32),
        ),
        in_specs=[anyspace, anyspace, vmem, anyspace, pl.BlockSpec(memory_space=pltpu.SMEM), vmem],
        out_specs=(vmem, pl.BlockSpec(memory_space=pltpu.SMEM)),
        scratch_shapes=[
            pltpu.VMEM((total, depth), bf),
            pltpu.VMEM((depth, cols), bf),
            pltpu.VMEM((depth, cols), f32),
            pltpu.VMEM((total, cols), bf),
            pltpu.VMEM((total, cols), bf),
            pltpu.VMEM((total // 2, cols), bf),
            pltpu.VMEM((2, 8 * max(CHUNKS), cols), f32),
            pltpu.VMEM((total // 2, cols), bf),
            pltpu.VMEM((2, 3, own, cols), bf),
            pltpu.VMEM((own, cols), bf),
            pltpu.VMEM((own, cols), bf),
            pltpu.VMEM((own, cols), f32),
            pltpu.VMEM((own, cols), bf),
            pltpu.VMEM((n, 8, 128), f32),
            pltpu.VMEM((n, 7, 8, 128), f32),
            pltpu.VMEM((8, 128), f32),
            pltpu.VMEM((15, 8, 128), f32),
            pltpu.VMEM((8, 128), f32),
            pltpu.VMEM((7, 8, 128), f32),
            dma, dma((n,)), dma((n,)), dma((RING,)),
            dma((n, max(AG_SEM) + 1)), dma((n, 2)), dma((n, 2)), dma((n,)), dma((n,)), dma((n,)),
            dma((n, 6)), dma((n,)), dma, dma,
        ],
        compiler_params=pltpu.CompilerParams(
            collective_id=0, has_side_effects=True, vmem_limit_bytes=54 * 1024 * 1024
        ),
    )(features, weight, norm_gain.reshape(1, cols), target, counts, counts.reshape(2, -1))
    return out, loss[0, 0]


def solution(mesh):
    placed = (P("grp", "tp"), P("tp", "grp"), P("grp"), P(None, "grp"), P())
    return jax.shard_map(
        shards, mesh=mesh, in_specs=placed, out_specs=(P("tp", "grp"), P()), check_vma=False
    )
```

time: 147 us -> 144 us (0.980)
  Pallas kernels: 142 us -> 138 us
    pallas_call x1, Pallas kernels: 142 us -> 138 us  [shards(): pl.pallas_call(functools.partial(kernel, cols * lax.axis_size('grp'), spl...]
where the time goes in v4:
time: 144 us; the launch traced here: 143 us
  Pallas kernels  138 us (96%)
  local copies, waits for them, and re-layouts  2.71 us (2%)
  between operations  2.33 us (2%)
    pallas_call x1, Pallas kernels, shards(): pl.pallas_call(functools.partial(kernel, cols * lax.axis_size('grp'), spl...  138 us

profile of v4, /device:TPU:1, one launch (start us, length us, event | category | flops | bytes accessed | tf_op | source)
XLA Modules:
  0.0 143.4 jit_solution(5888833718313488212)
XLA Ops:
  0.6 138.4 %shard_map.68 = (bf16[3072,1024]{1,0:T(8,128)(2,1)S(1)}, f32[1,1]{1,0:T(1,128)}) custom-call(bf16[256,3072]{1,0:T(8,128)(2,1)} %features.1, bf16[3072,1024]{1,0:T(8,128)(2,1)} %weight.1, f32[1,1024]{1,0:T(1,128)} %bitcast.3, bf16[2048,1024]{1,0:T(8,128)(2,1)} %target.1, s32[256]{0:T(256)} %counts_s.1, s32[2,128]{1,0:T(2,128)} %bitcast.4), custom_call_target="tpu_custom_call" | custom-call | tf_op jit(solution)/shard_map/pallas_call | solution.py:450
  139.0 2.7 %copy.9 = bf16[3072,1024]{1,0:T(8,128)(2,1)} copy(bf16[3072,1024]{1,0:T(8,128)(2,1)S(1)} %get-tuple-element.6) | data formatting | bytes 12582912

commit v5 on v4

--- a/solution.py
+++ b/solution.py
@@ -39,6 +39,7 @@
     ("d", 3, 3), ("d", 4, 0), ("d", 4, 1), ("d", 4, 2), ("d", 4, 3),
 )
 TILE = 256
+WIDE = 512
 RING = 64
 AG_SEM = (0, 1, 2, 3, 4, 5, 6, 7, 8, 8, 3, 3, 3, 9, 10)
 MESH = pl.DeviceIdType.MESH
@@ -363,7 +364,7 @@
         r4 = 4 * CHUNKS[c]
         arrived(gbuf.at[pl.ds(pl.multiple_of(8 * offs[c] + (1 - core) * r4, 16), r4), :], gp_r.at[c])
 
-    n_tiles = depth // TILE
+    n_tiles = depth // WIDE
     last = n_chunks - 1
 
     def outer(i, part):
@@ -373,7 +374,7 @@
         rows = pl.ds(8 * offs[GROUPS[i][0]], 8 * sum(CHUNKS[c] for c in GROUPS[i]))
 
         def tile(j, _):
-            k = pl.ds(pl.multiple_of(j * TILE, TILE), TILE)
+            k = pl.ds(pl.multiple_of(j * WIDE, WIDE), WIDE)
             turned = jnp.transpose(fbuf[rows, k])
             for n in range(n_cols):
                 col = pl.ds(n * TILE, TILE)

time: 144 us -> 140 us (0.972)
  Pallas kernels: 138 us -> 135 us
    pallas_call x1, Pallas kernels: 138 us -> 135 us  [shards(): pl.pallas_call(functools.partial(kernel, cols * lax.axis_size('grp'), spl...]
where the time goes in v5:
time: 140 us
  Pallas kernels  135 us (96%)
  local copies, waits for them, and re-layouts  2.71 us (2%)
  between operations  2.33 us (2%)
    pallas_call x1, Pallas kernels, shards(): pl.pallas_call(functools.partial(kernel, cols * lax.axis_size('grp'), spl...  135 us

profile of v5, /device:TPU:1, one launch (start us, length us, event | category | flops | bytes accessed | tf_op | source)
XLA Modules:
  0.0 140.3 jit_solution(13247583800199263245)
XLA Ops:
  0.6 135.2 %shard_map.68 = (bf16[3072,1024]{1,0:T(8,128)(2,1)S(1)}, f32[1,1]{1,0:T(1,128)}) custom-call(bf16[256,3072]{1,0:T(8,128)(2,1)} %features.1, bf16[3072,1024]{1,0:T(8,128)(2,1)} %weight.1, f32[1,1024]{1,0:T(1,128)} %bitcast.3, bf16[2048,1024]{1,0:T(8,128)(2,1)} %target.1, s32[256]{0:T(256)} %counts_s.1, s32[2,128]{1,0:T(2,128)} %bitcast.4), custom_call_target="tpu_custom_call" | custom-call | tf_op jit(solution)/shard_map/pallas_call | solution.py:451
  135.9 2.7 %copy.9 = bf16[3072,1024]{1,0:T(8,128)(2,1)} copy(bf16[3072,1024]{1,0:T(8,128)(2,1)S(1)} %get-tuple-element.6) | data formatting | bytes 12582912

commit v6 on v5

--- a/solution.py
+++ b/solution.py
@@ -413,14 +413,14 @@
     for step, c, part in ORDER:
         if (step, c, part) == ("m1", 0, 0):
             w_cp.wait()
+        if (step, c, part) == ("d", len(GROUPS) - 1, 0):
+            pass_loss()
         if step in parted:
             parted[step](c, part)
         else:
             steps[step](c)
         if (step, c) == ("g", last):
             share_loss()
-        if (step, c, part) == ("x", last, 0):
-            pass_loss()
         if (step, c) == ("fin", last):
             gathering = False
         for _ in range(4 if gathering else 2):

time: 140 us -> 140 us (level)
  no operation moved by 1% of the time
where the time goes in v6:
time: 140 us; the launch traced here: 139 us
  Pallas kernels  134 us (96%)
  local copies, waits for them, and re-layouts  2.71 us (2%)
  between operations  2.33 us (2%)
    pallas_call x1, Pallas kernels, shards(): pl.pallas_call(functools.partial(kernel, cols * lax.axis_size('grp'), spl...  134 us

profile of v6, /device:TPU:1, one launch (start us, length us, event | category | flops | bytes accessed | tf_op | source)
XLA Modules:
  0.0 138.9 jit_solution(4494091463901648955)
XLA Ops:
  0.6 133.9 %shard_map.68 = (bf16[3072,1024]{1,0:T(8,128)(2,1)S(1)}, f32[1,1]{1,0:T(1,128)}) custom-call(bf16[256,3072]{1,0:T(8,128)(2,1)} %features.1, bf16[3072,1024]{1,0:T(8,128)(2,1)} %weight.1, f32[1,1024]{1,0:T(1,128)} %bitcast.3, bf16[2048,1024]{1,0:T(8,128)(2,1)} %target.1, s32[256]{0:T(256)} %counts_s.1, s32[2,128]{1,0:T(2,128)} %bitcast.4), custom_call_target="tpu_custom_call" | custom-call | tf_op jit(solution)/shard_map/pallas_call | solution.py:451
  134.5 2.7 %copy.9 = bf16[3072,1024]{1,0:T(8,128)(2,1)} copy(bf16[3072,1024]{1,0:T(8,128)(2,1)S(1)} %get-tuple-element.6) | data formatting | bytes 12582912
